TPU v7x, 128 devices: a whole 4x4x4 slice. The times are simulated.
128 devices in a mesh: sky: 32 (over y, z, core), band: 4 (over x).
Axes of the slice: x: 4, y: 4, z: 4, core: 2. Of those that a mesh axis runs over, the one named last changes fastest.
Arguments:
- exposures: bfloat16 [32, 4, 1024, 1024], P('sky', 'band'), may hold values from -6 to 6
- inv_variance: bfloat16 [32, 4, 1024, 1024], P('sky', 'band'), may hold values from 0.25 to 4
- mask_planes: int32 [32, 4, 2, 35], P('sky', 'band'), may hold values from 0 to 1073741823, as said below
- sky_columns: int32 [32, 4, 8], replicated, may hold values from 0 to 31, as said below
- basis_rows: float32 [9, 25], replicated, may hold values from -1 to 1
- basis_cols: float32 [9, 25], replicated, may hold values from -1 to 1
- match_coeffs: float32 [32, 4, 9], P('sky', 'band'), may hold values from -2 to 2
- detect_taps: float32 [4, 31], P('band'), may hold values from 0.05 to 0.3
Outputs:
- difference: bfloat16 [32, 4, 1024, 1024], P('sky', 'band')
- detection: float32 [1024, 4096], P('band', 'sky')
Inputs may be any that keep to these rules, and one draw needn't show every extreme that they name: Each row sky_columns[e, b] holds 8 consecutive sky tile columns in order, counted modulo 32; every sky tile column is covered by some exposure of every band. Bit j of mask_planes[e, b, 0, w] marks pixel column 30 w + j of that exposure as bad and bit j of mask_planes[e, b, 1, w] pixel row 30 w + j; bits past 1024 are ignored. In every draw some word has all 30 bits set.
All inputs are finite; a program needn't handle non-finite values.
Results may differ from a plain program's by a relative error of at most 0.0095.
Values may be sent and summed in bfloat16 or wider, within the bound.
A program may use at most 128 MiB of HBM per device.

v0:
```python
import jax
import jax.numpy as jnp
from jax import lax
from jax.sharding import PartitionSpec as P

TILE = 128
NB = 9
TAPS = 25
DTAPS = 31


def with_halo(block, sides, width):
    for axis, dim in sides:
        count = lax.axis_size(axis)
        forward = [(i, i + 1) for i in range(count - 1)]
        forward.append((count - 1, 0))
        backward = [(target, source) for source, target in forward]
        low = lax.ppermute(
            lax.slice_in_dim(block, block.shape[dim] - width, None, axis=dim), axis, forward
        )
        high = lax.ppermute(lax.slice_in_dim(block, 0, width, axis=dim), axis, backward)
        block = jnp.concatenate([low, block, high], axis=dim)
    return block


def cut_along(value, dim, length):
    dims = value.shape
    pieces = value.reshape(*dims[:dim], length, dims[dim] // length, *dims[dim + 1 :])
    return jnp.moveaxis(pieces, dim, 0)


def sum_at_owner(value, axis, dim):
    pieces = cut_along(value, dim, lax.axis_size(axis))
    arrived = lax.all_to_all(pieces, axis, split_axis=0, concat_axis=0, tiled=True)
    return arrived.sum(axis=0)


def band_matrix(tap_rows, window_width):
    offsets = (
        jnp.arange(window_width, dtype=jnp.int32)[:, None]
        - jnp.arange(TILE, dtype=jnp.int32)[None, :]
    )
    selector = (
        offsets[:, :, None] == jnp.arange(tap_rows.shape[1], dtype=jnp.int32)[None, None, :]
    ).astype(jnp.float32)
    return jnp.einsum(
        "wtl,kl->kwt", selector, tap_rows.astype(jnp.float32), precision=lax.Precision.HIGHEST
    ).astype(jnp.bfloat16)


def keep_pixels(planes, side_length):
    places = jnp.arange(side_length, dtype=jnp.int32)
    column_bits = jnp.bitwise_and(jnp.right_shift(planes[0][places // 30], places % 30), 1)
    row_bits = jnp.bitwise_and(jnp.right_shift(planes[1][places // 30], places % 30), 1)
    return jnp.logical_and(row_bits[:, None] == 0, column_bits[None, :] == 0)


def psf_match(picture, column_taps, row_taps):
    side_length = picture.shape[1]
    block_count = side_length // TILE
    margin = TAPS // 2
    width_full = TILE + 2 * margin
    padded = jnp.pad(picture, ((0, 0), (margin, margin)))
    blocks = jnp.stack(
        [
            padded[:, TILE * block_index : TILE * block_index + width_full]
            for block_index in range(block_count)
        ],
        0,
    )
    column_band = band_matrix(column_taps, width_full)
    column_pass = jnp.einsum(
        "jyw,kwt->kyjt", blocks, column_band, preferred_element_type=jnp.float32
    )
    column_pass = column_pass.reshape(NB, side_length, side_length).astype(jnp.bfloat16)
    row_padded = jnp.pad(column_pass, ((0, 0), (margin, margin), (0, 0)))
    row_blocks = jnp.stack(
        [
            row_padded[:, TILE * block_index : TILE * block_index + width_full, :]
            for block_index in range(block_count)
        ],
        0,
    )
    row_band = band_matrix(row_taps, width_full)
    summed = jnp.einsum("ikwx,kwt->itx", row_blocks, row_band, preferred_element_type=jnp.float32)
    return summed.reshape(side_length, side_length).astype(jnp.bfloat16)


def average_pieces(pieces):
    matched_in, weight_in = pieces
    weight_float = weight_in.astype(jnp.float32)
    numer = jnp.sum(weight_float * matched_in.astype(jnp.float32), axis=1)
    denom = jnp.sum(weight_float, axis=1)
    return (numer / jnp.maximum(denom, 1.0)).astype(jnp.bfloat16)


def subtract_template(template, matched, own_columns, side_length, sky_count):
    gathered = lax.all_gather(template, "sky", axis=1, tiled=True).reshape(
        side_length, sky_count, TILE
    )
    picked = jnp.take(gathered, own_columns, axis=1).reshape(side_length, side_length)
    return (matched.astype(jnp.float32) - picked.astype(jnp.float32)).astype(jnp.bfloat16)


def body(
    exposures,
    inv_variance,
    mask_planes,
    sky_columns,
    basis_rows,
    basis_cols,
    match_coeffs,
    detect_taps,
):
    picture = exposures[0, 0]
    side_length = picture.shape[0]
    block_count = side_length // TILE
    sky_count = lax.axis_size("sky")
    own_sky = lax.axis_index("sky")
    own_band = lax.axis_index("band")
    column_taps = (match_coeffs[0, 0][:, None] * basis_cols).astype(jnp.bfloat16)
    matched = psf_match(picture, column_taps, basis_rows.astype(jnp.bfloat16))
    keep = keep_pixels(mask_planes[0, 0], side_length)
    variance_inv = inv_variance[0, 0]
    weight = jnp.where(keep, variance_inv, jnp.zeros_like(variance_inv))
    own_columns = sky_columns[own_sky, own_band]
    empty_slots = jnp.zeros((side_length, sky_count, TILE), jnp.bfloat16)
    send_matched = empty_slots.at[:, own_columns, :].set(
        matched.reshape(side_length, block_count, TILE)
    )
    send_weight = empty_slots.at[:, own_columns, :].set(
        weight.reshape(side_length, block_count, TILE)
    )
    template = average_pieces(
        (
            lax.all_to_all(send_matched, "sky", split_axis=1, concat_axis=1, tiled=True),
            lax.all_to_all(send_weight, "sky", split_axis=1, concat_axis=1, tiled=True),
        )
    )
    difference = subtract_template(template, matched, own_columns, side_length, sky_count)
    margin = DTAPS // 2
    width_full = TILE + 2 * margin
    filter_band = band_matrix(detect_taps.astype(jnp.bfloat16), width_full)[0]
    widened = with_halo(template, (("sky", 1),), margin)
    smoothed = jnp.dot(widened, filter_band, preferred_element_type=jnp.float32).astype(
        jnp.bfloat16
    )
    smooth_padded = jnp.pad(smoothed, ((margin, margin), (0, 0)))
    smooth_blocks = jnp.stack(
        [
            smooth_padded[TILE * block_index : TILE * block_index + width_full]
            for block_index in range(block_count)
        ],
        0,
    )
    filtered = jnp.einsum(
        "iwx,wt->itx", smooth_blocks, filter_band, preferred_element_type=jnp.float32
    ).reshape(side_length, TILE)
    power = filtered * filtered
    detection = sum_at_owner(power, "band", 0)
    return (difference[None, None], detection)


def solution(mesh):
    in_specs = (
        P("sky", "band", None, None),
        P("sky", "band", None, None),
        P("sky", "band", None, None),
        P(),
        P(),
        P(),
        P("sky", "band", None),
        P("band", None),
    )
    out_specs = (P("sky", "band", None, None), P("band", "sky"))
    return jax.shard_map(body, mesh=mesh, in_specs=in_specs, out_specs=out_specs, check_vma=False)
```

profile of v0, /device:TPU:24, one launch (start us, length us, event | category | flops | bytes accessed | tf_op | source)
XLA Modules:
  0.0 442.6 jit_solution(8928743750772134446)
XLA Ops:
  7.2 2.9 copy.63
  11.6 9.2 %convolution_convert_fusion = bf16[9,128,8,1024]{3,1,2,0:T(8,128)(2,1)} fusion(bf16[8,1024,152]{1,2,0:T(8,128)(2,1)S(1)} %fusion.34, bf16[9,152,128,1]{2,0,1,3:T(8,128)(2,1)S(1)} %fusion.19), kind=kOutput, calls=%fused_computation.8 | convolution fusion | flops 2878341120 | bytes 21714944 | tf_op jit(solution)/shard_map/jyw,kwt->kyjt/dot_general | solution.py:72
  20.8 24.6 %copy.65 = bf16[9,1024,1024]{2,1,0:T(8,128)(2,1)} copy(bf16[9,1024,1024]{1,2,0:T(8,128)(2,1)} %bitcast.238) | data formatting | bytes 37748736 | tf_op jit(solution)/shard_map/convert_element_type | solution.py:75
  45.4 4.3 fusion.2
  49.8 3.8 copy-done.2
  53.6 2.5 fusion.10
  58.5 2.5 fusion.8
  61.0 2.5 fusion.7
  71.4 9.9 %bitcast_convert_fusion = bf16[128,8,1024]{2,0,1:T(8,128)(2,1)S(1)} fusion(bf16[8,9,152,1024]{3,2,1,0:T(8,128)(2,1)} %fusion.4, bf16[9,152,128]{2,0,1:T(8,128)(2,1)S(1)} %fusion.20), kind=kOutput, calls=%fused_computation.9 | convolution fusion | flops 2869952512 | bytes 24860672 | tf_op jit(solution)/shard_map/ikwx,kwt->itx/dot_general | solution.py:85
  83.8 5.1 %broadcast_in_dim.18.clone.1 = bf16[1024,32,128]{2,0,1:T(8,128)(2,1)} broadcast(bf16[]{:T(256)} %constant.31.clone.1), dimensions={} | broadcast | bytes 8388610 | tf_op jit(solution)/shard_map/broadcast_in_dim | solution.py:127
  88.9 5.7 %scatter_fusion.1 = bf16[1024,32,128]{2,0,1:T(8,128)(2,1)} fusion(bf16[1024,32,128]{2,0,1:T(8,128)(2,1)} %broadcast_in_dim.18.clone.1, s32[8]{0:T(128)S(1)} %fusion.61, bf16[8,1024,128]{2,1,0:T(8,128)(2,1)} %bitcast.250), kind=kCustom, calls=%fused_computation.2 | custom fusion | bytes 6291488 | tf_op jit(solution)/shard_map/scatter | solution.py:128
  94.6 8.4 %all-to-all-start.1 = ((bf16[1024,32,128]{2,0,1:T(8,128)(2,1)}), bf16[1024,32,128]{2,0,1:T(8,128)(2,1)}, u32[]{:S(2)}, u32[]{:S(2)}) async-start(bf16[1024,32,128]{2,0,1:T(8,128)(2,1)} %scatter_fusion.1), calls=%async_computation.1 | async-start | bytes 16777216 | tf_op jit(solution)/shard_map/all_to_all | solution.py:136
  107.9 4.5 %compare_select_fusion.2 = s32[1024,1]{0,1:T(1,128)S(1)} fusion(s32[]{:T(128)} %bitcast.97, s32[]{:T(128)} %bitcast.98, s32[]{:T(128)} %bitcast.99, s32[]{:T(128)} %bitcast.100, s32[]{:T(128)} %bitcast.101, s32[]{:T(128)} %bitcast.103, s32[]{:T(128)} %bitcast.102), kind=kLoop, calls=%fused_computation.125 | loop fusion | flops 23552 | bytes 4124 | tf_op jit(solution)/shard_map/gather | solution.py:53
  113.8 4.4 %compare_select_fusion.1 = s32[1024,1]{0,1:T(1,128)S(1)} fusion(s32[]{:T(128)} %bitcast.61, s32[]{:T(128)} %bitcast.62, s32[]{:T(128)} %bitcast.63, s32[]{:T(128)} %bitcast.64, s32[]{:T(128)} %bitcast.65, s32[]{:T(128)} %bitcast.67, s32[]{:T(128)} %bitcast.66), kind=kLoop, calls=%fused_computation.124 | loop fusion | flops 23552 | bytes 4124 | tf_op jit(solution)/shard_map/gather | solution.py:54
  118.3 17.3 %fusion.49 = pred[8,128]{1,0:T(8,128)(4,1)S(1)} fusion(pred[1024]{0:T(1024)(128)(4,1)S(1)} %compare_reduce_fusion, pred[1024]{0:T(1024)(128)(4,1)S(1)} %compare_reduce_fusion.1, pred[1024]{0:T(1024)(128)(4,1)S(1)} %compare_reduce_fusion.2, pred[1024]{0:T(1024)(128)(4,1)S(1)} %compare_reduce_fusion.3, pred[1024]{0:T(1024)(128)(4,1)S(1)} %compare_reduce_fusion.4, ...), kind=kLoop, calls=%fused_computation.147 | loop fusion | flops 39936 | bytes 33904 | tf_op jit(solution)/shard_map/eq | solution.py:55
  135.6 17.6 %fusion.46 = pred[1024]{0:T(1024)(128)(4,1)S(1)} fusion(pred[1024]{0:T(1024)(128)(4,1)S(1)} %compare_reduce_fusion, pred[1024]{0:T(1024)(128)(4,1)S(1)} %compare_reduce_fusion.1, pred[1024]{0:T(1024)(128)(4,1)S(1)} %compare_reduce_fusion.2, pred[1024]{0:T(1024)(128)(4,1)S(1)} %compare_reduce_fusion.3, pred[1024]{0:T(1024)(128)(4,1)S(1)} %compare_reduce_fusion.4, ...), kind=kLoop, calls=%fused_computation.144 | loop fusion | flops 37888 | bytes 33904 | tf_op jit(solution)/shard_map/eq | solution.py:55
  155.2 5.1 %broadcast_in_dim.18.clone = bf16[1024,32,128]{2,0,1:T(8,128)(2,1)} broadcast(bf16[]{:T(256)} %constant.31.clone.1), dimensions={} | broadcast | bytes 8388610 | tf_op jit(solution)/shard_map/broadcast_in_dim | solution.py:127
  160.3 5.7 %scatter_fusion = bf16[1024,32,128]{2,0,1:T(8,128)(2,1)} fusion(bf16[1024,32,128]{2,0,1:T(8,128)(2,1)} %broadcast_in_dim.18.clone, s32[8]{0:T(128)S(1)} %fusion.61, bf16[8,1024,128]{2,1,0:T(8,128)(2,1)} %fusion.16), kind=kCustom, calls=%fused_computation.1 | custom fusion | bytes 6291488 | tf_op jit(solution)/shard_map/scatter | solution.py:131
  166.1 41.3 %all-to-all-done.1 = bf16[1024,32,128]{2,0,1:T(8,128)(2,1)} async-done(((bf16[1024,32,128]{2,0,1:T(8,128)(2,1)}), bf16[1024,32,128]{2,0,1:T(8,128)(2,1)}, u32[]{:S(2)}, u32[]{:S(2)}) %all-to-all-start.1) | async-done | bytes 8388640 | tf_op jit(solution)/shard_map/all_to_all | solution.py:136
  207.4 119.7 %all_to_all.15 = bf16[1024,32,128]{2,0,1:T(8,128)(2,1)} all-to-all(bf16[1024,32,128]{2,0,1:T(8,128)(2,1)} %scatter_fusion), channel_id=1, replica_groups=mesh['sky'=32,'band'=4] {'sky'}, dimensions={1} | all-to-all | bytes 16777216 | tf_op jit(solution)/shard_map/all_to_all | solution.py:137
  327.0 9.0 %convert_reduce_fusion = (f32[1024,128]{1,0:T(8,128)S(1)}, f32[1024,128]{1,0:T(8,128)S(1)}) fusion(bf16[1024,32,128]{2,0,1:T(8,128)(2,1)} %all_to_all.15, bf16[1024,32,128]{2,0,1:T(8,128)(2,1)} %all-to-all-done.1), kind=kLoop, calls=%fused_computation.3 | loop fusion | flops 20709376 | bytes 17825792 | tf_op jit(solution)/shard_map/reduce_sum | solution.py:93
  338.0 3.8 collective-permute-start.1
  341.9 3.0 copy.78
  348.6 4.3 all-to-all-start.2
  353.0 8.0 %all-to-all-done.2 = f32[4,256,128]{2,1,0:T(8,128)S(1)} async-done(((f32[4,256,128]{2,1,0:T(8,128)}), f32[4,256,128]{2,1,0:T(8,128)S(1)}, u32[]{:S(2)}, u32[]{:S(2)}) %all-to-all-start.2) | async-done | bytes 524320 | tf_op jit(solution)/shard_map/all_to_all | solution.py:34
  361.7 33.8 %all-gather.2.cloned.1.call-done = bf16[1024,4096]{1,0:T(8,128)(2,1)} async-done(((bf16[1024,128]{1,0:T(8,128)(2,1)}), bf16[1024,4096]{1,0:T(8,128)(2,1)}) %all-gather.2.cloned.1.call-update) | async-done | bytes 8388624 | tf_op jit(solution)/shard_map/all_gather | solution.py:98
  395.5 11.9 %copy.75 = bf16[1024,4096]{0,1:T(8,128)(2,1)} copy(bf16[1024,4096]{1,0:T(8,128)(2,1)} %all-gather.2.cloned.1.call-done) | data formatting | bytes 16777216 | tf_op jit(solution)/shard_map/all_gather | solution.py:98
  407.4 11.9 %copy.76 = bf16[1024,32,128]{2,0,1:T(8,128)(2,1)} copy(bf16[1024,32,128]{0,2,1:T(8,128)(2,1)} %bitcast.239) | data formatting | bytes 16777216 | tf_op jit(solution)/shard_map/reshape | solution.py:98
  419.3 5.5 %gather_fusion = bf16[8,1024,128]{2,1,0:T(8,128)(2,1)} fusion(bf16[1024,32,128]{2,0,1:T(8,128)(2,1)} %copy.76, s32[1024]{0:T(1024)S(1)} %pad_clamp_fusion), kind=kCustom, calls=%fused_computation | custom fusion | bytes 4194336 | tf_op jit(solution)/shard_map/jit(_take)/gather | solution.py:101
  424.8 2.9 copy.77
  427.7 4.1 subtract_convert_fusion
  431.8 3.9 copy.79
  (94 shorter events, 28.9 us)
Async XLA Ops:
  7.2 76.4 %copy-start = (s32[32,4,8]{0,2,1:T(8,128)S(1)}, s32[32,4,8]{0,2,1:T(8,128)}, u32[]{:S(2)}) copy-start(s32[32,4,8]{0,2,1:T(8,128)} %param.11) | copy-start | bytes 12292
  10.3 0.7 copy-start.5
  10.3 0.7 copy-start.6
  45.4 8.2 %copy-start.2 = (bf16[9,1024,1024]{2,1,0:T(8,128)(2,1)S(1)}, bf16[9,1024,1024]{2,1,0:T(8,128)(2,1)}, u32[]{:S(2)}) copy-start(bf16[9,1024,1024]{2,1,0:T(8,128)(2,1)} %copy.65) | copy-start | bytes 56623108
  68.4 2.4 copy-start.7
  94.6 112.8 %all-to-all-start.1 = ((bf16[1024,32,128]{2,0,1:T(8,128)(2,1)}), bf16[1024,32,128]{2,0,1:T(8,128)(2,1)}, u32[]{:S(2)}, u32[]{:S(2)}) async-start(bf16[1024,32,128]{2,0,1:T(8,128)(2,1)} %scatter_fusion.1), calls=%async_computation.1 | async-start | bytes 16777216 | tf_op jit(solution)/shard_map/all_to_all | solution.py:136
  103.0 3.4 copy-start.4
  103.1 292.4 %all-gather.2.cloned.1.call-start = ((), (), s32[]{:S(2)}) async-start(), calls=%async_computation.3 | async-start | bytes 8650752 | tf_op jit(solution)/shard_map/all_gather | solution.py:98
  327.0 10.2 %copy-start.8 = (f32[1,31]{1,0:T(1,128)S(1)}, f32[1,31]{1,0:T(1,128)}, u32[]{:S(2)}) copy-start(f32[1,31]{1,0:T(1,128)} %param.15) | copy-start | bytes 376
  336.9 0.9 copy-start.3
  338.0 8.0 %collective-permute-start = (bf16[1024,15]{1,0:T(8,128)(2,1)S(1)}, bf16[1024,15]{1,0:T(8,128)(2,1)S(1)}, u32[]{:S(2)}, u32[]{:S(2)}) collective-permute-start(bf16[1024,15]{1,0:T(8,128)(2,1)S(1)} %get-tuple-element.10), channel_id=1, source_target_pairs={{0,4},{4,8},{8,12},{12,16},{16,20},{20,24},{24,28},{28,32},{32,36}... | collective-permute-start | bytes 92168 | tf_op jit(solution)/shard_map/ppermute | solution.py:18
  338.0 7.9 %collective-permute-start.1 = (bf16[1024,15]{1,0:T(8,128)(2,1)S(1)}, bf16[1024,15]{1,0:T(8,128)(2,1)}, u32[]{:S(2)}, u32[]{:S(2)}) collective-permute-start(bf16[1024,15]{1,0:T(8,128)(2,1)S(1)} %get-tuple-element.11), channel_id=1, source_target_pairs={{4,0},{8,4},{12,8},{16,12},{20,16},{24,20},{28,24},{32,28},{36,32}... | collective-permute-start | bytes 92168 | tf_op jit(solution)/shard_map/ppermute | solution.py:21
  348.6 12.4 %all-to-all-start.2 = ((f32[4,256,128]{2,1,0:T(8,128)}), f32[4,256,128]{2,1,0:T(8,128)S(1)}, u32[]{:S(2)}, u32[]{:S(2)}) async-start(f32[4,256,128]{2,1,0:T(8,128)} %bitcast.124), calls=%async_computation.2 | async-start | bytes 1048576 | tf_op jit(solution)/shard_map/all_to_all | solution.py:34
  427.7 8.1 %copy-start.1 = (s32[32,4,8]{0,2,1:T(8,128)S(1)}, s32[32,4,8]{0,2,1:T(8,128)}, u32[]{:S(2)}) copy-start(s32[32,4,8]{0,2,1:T(8,128)} %param.11) | copy-start | bytes 12292
Sparse Core Ops, SparseCore 0:
  337.0 58.3 all-gather.1
where the time goes:
time: 447 us; the launch traced here: 443 us
  local copies, waits for them, and re-layouts  123 us (28%)
  blocking collectives  120 us (27%)
  waiting for transfers between devices  84.1 us (19%)
  other arithmetic  61.9 us (14%)
  matrix products  23.3 us (5%)
  starting transfers between devices  16.7 us (4%)
  between operations  14.3 us (3%)
    all_to_all x1, blocking collectives, body(): lax.all_to_all(send_weight, 'sky', split_axis=1, concat_axis=1, tiled=True)  120 us
    all_to_all x1, waiting for transfers between devices, body(): lax.all_to_all(send_matched, 'sky', split_axis=1, concat_axis=1, tiled=True)  41.3 us
    eq x2, other arithmetic, keep_pixels(): return jnp.logical_and(row_bits[:, None] == 0, column_bits[None, :] == 0)  34.9 us
    all_gather x1, waiting for transfers between devices, subtract_template(): lax.all_gather(template, 'sky', axis=1, tiled=True)  33.8 us
    unnamed x43, local copies, waits for them, and re-layouts  33.6 us
    convert_element_type x1, local copies, waits for them, and re-layouts, psf_match(): column_pass.reshape(NB, side_length, side_length).astype(jnp.bfloat16)  24.6 us
    all_gather x1, local copies, waits for them, and re-layouts, subtract_template(): lax.all_gather(template, 'sky', axis=1, tiled=True)  11.9 us
    reshape x1, local copies, waits for them, and re-layouts, subtract_template(): lax.all_gather(template, 'sky', axis=1, tiled=True)  11.9 us
  transfers between devices with their start and end apart: 5, of which 4 were waited for; matrix products, arithmetic and copies ran while one was open for 16% of the time, Pallas kernels for 0%

commit v1 on v0

v1 whole, which is shorter than its diff:
```python
import jax
import jax.numpy as jnp
from jax import lax
from jax.experimental import pallas as pl
from jax.experimental.pallas import tpu as pltpu
from jax.sharding import PartitionSpec as P

TILE = 128
NB = 9
TAPS = 25
DTAPS = 31
IMG = 1024
HALO = 12
STRIP = NB * 16
KROWS = 10 * STRIP
NCHUNK = 8
MESH = pl.DeviceIdType.MESH
F32 = jnp.float32
BF16 = jnp.bfloat16


def rows_of(block):
    return pl.ds(pl.multiple_of(block * TILE, TILE), TILE)


def lanes_of(block):
    return pl.ds(pl.multiple_of(block * TILE, TILE), TILE)


def device_of(half, klass, slot):
    first = 8 * slot + klass
    second = 8 * lax.div(klass, 2) + 2 * slot + lax.rem(klass, 2)
    return jnp.where(half == 0, first, second)


def place(half):
    own = lax.axis_index("sky")
    y, rest = lax.div(own, 8), lax.rem(own, 8)
    z, core = lax.div(rest, 2), lax.rem(rest, 2)
    klass = jnp.where(half == 0, rest, 2 * y + core)
    slot = jnp.where(half == 0, y, z)
    return klass, slot


def row_block(step):
    half = lax.rem(step, 2)
    return half, lax.div(step, 2) + 4 * half


def turned(tiles, amount):
    for bit in (1, 2, 4):
        take = jnp.bitwise_and(jnp.full(tiles[0].shape, amount, jnp.int32), bit) != 0
        tiles = [jnp.where(take, tiles[(i + bit) % 8], tiles[i]) for i in range(8)]
    return tiles


def bit_lanes(planes_ref, plane):
    lane = lax.broadcasted_iota(jnp.int32, (8, IMG), 1)
    word = jnp.zeros((8, IMG), jnp.int32)
    first = jnp.zeros((8, IMG), jnp.int32)
    for index in range(35):
        inside = lane >= 30 * index
        word = jnp.where(inside, planes_ref[plane, index], word)
        first = jnp.where(inside, 30 * index, first)
    bit = jnp.bitwise_and(lax.shift_right_logical(word, lane - first), 1)
    return (1 - bit).astype(F32)


def build_taps(cols_ref, rows_ref, coeff_ref, col_mat, row_mat):
    pad = jnp.zeros((1, TILE - TAPS), F32)
    far = jnp.zeros((1, TILE), F32)
    for k in range(NB):
        taps = (cols_ref[k : k + 1, :] * coeff_ref[0, k]).astype(BF16).astype(F32)
        base = pltpu.roll(jnp.concatenate([taps, pad, far], 1), 2 * TILE - HALO, 1)
        ring = pltpu.roll(jnp.broadcast_to(base, (TILE, 2 * TILE)), 0, 1, stride=1, stride_axis=0)
        col_mat[:, k * TILE : (k + 1) * TILE] = ring.T.astype(BF16)
    place_w = lax.broadcasted_iota(jnp.int32, (TILE, 512), 0)
    place_l = lax.broadcasted_iota(jnp.int32, (TILE, 512), 1)
    picker = jnp.where(
        jnp.logical_and(place_l == lax.div(place_w, 16) * STRIP + lax.rem(place_w, 16), place_w < 48),
        1.0,
        0.0,
    ).astype(BF16)
    stacked = []
    for k in range(NB):
        taps = rows_ref[k : k + 1, :].astype(BF16).astype(F32)
        base = pltpu.roll(jnp.concatenate([taps, pad], 1), 4, 1)
        stacked.append(pltpu.roll(jnp.broadcast_to(base, (16, TILE)), 0, 1, stride=1, stride_axis=0))
    spread = jnp.dot(
        jnp.concatenate(stacked, 0).astype(BF16), picker, preferred_element_type=F32
    )
    first = jnp.zeros((16, 512), F32)
    for k in range(NB):
        first = first + pltpu.roll(spread[16 * k : 16 * k + 16], 16 * k, 1)
    first = jnp.concatenate([first, jnp.zeros((16, 1024), F32)], 1)
    for u in range(8):
        row_mat[16 * u : 16 * u + 16, :] = pltpu.roll(first, STRIP * u, 1)[:, :KROWS].astype(BF16)


def column_pass(picture, col_mat, mid):
    mid[0] = jnp.zeros((NB, 16, IMG), BF16)
    mid[65] = jnp.zeros((NB, 16, IMG), BF16)
    near = lax.broadcasted_iota(jnp.int32, (IMG, TILE), 1) < 64

    def one(j, _):
        here = picture[:, lanes_of(j)]
        after = picture[:, lanes_of(jnp.minimum(j + 1, 7))]
        before = picture[:, lanes_of(jnp.maximum(j - 1, 0))]
        zero = jnp.zeros_like(here)
        after = jnp.where(jnp.broadcast_to(j < 7, near.shape), after, zero)
        before = jnp.where(jnp.broadcast_to(j > 0, near.shape), before, zero)
        lhs = jnp.concatenate([here, jnp.where(near, after, before)], 1)
        for k in range(0, NB, 2):
            count = min(2, NB - k)
            got = jnp.dot(
                lhs, col_mat[:, k * TILE : (k + count) * TILE], preferred_element_type=F32
            ).astype(BF16)
            for t in range(count):
                mid[1:65, k + t, :, lanes_of(j)] = got[:, t * TILE : (t + 1) * TILE].reshape(64, 16, TILE)
        return 0

    lax.fori_loop(0, 8, one, 0)


def coadd_kernel(
    picture_in,
    variance_in,
    planes_ref,
    sky_ref,
    rows_ref,
    cols_ref,
    coeff_ref,
    difference_out,
    template_out,
    picture,
    variance,
    col_keep,
    row_keep,
    col_mat,
    row_mat,
    mid,
    matched,
    w_send,
    w_recv,
    m_send,
    m_recv,
    p_send,
    p_recv,
    numer_own,
    denom_own,
    t_all,
    q_send,
    q_recv,
    flat_ref,
    d_out,
    load_sem,
    out_sem,
    send_sem,
    w_sem,
    m_sem,
    p_sem,
    t_sem,
    q_sem,
):
    own = lax.axis_index("sky")
    band = lax.axis_index("band")
    barrier = pltpu.get_barrier_semaphore()
    for half in range(2):
        klass, slot = place(half)
        for d in range(1, 8):
            peer = device_of(half, lax.rem(klass + d, 8), slot)
            pl.semaphore_signal(barrier, inc=1, device_id=(peer, band), device_id_type=MESH)
    load_variance = pltpu.make_async_copy(variance_in, variance, load_sem.at[0])
    load_picture = pltpu.make_async_copy(picture_in, picture, load_sem.at[1])
    load_variance.start()
    load_picture.start()
    start = sky_ref[own, band, 0]
    col_keep[...] = bit_lanes(planes_ref, 0)
    row_keep[...] = bit_lanes(planes_ref, 1)
    load_variance.wait()
    pl.semaphore_wait(barrier, 14)

    def send(src, dst, sem_send, sem_recv, device):
        pltpu.make_async_remote_copy(
            src_ref=src,
            dst_ref=dst,
            send_sem=sem_send,
            recv_sem=sem_recv,
            device_id=(device, band),
            device_id_type=MESH,
        ).start()

    def wait_for(ref, sem):
        pltpu.make_async_copy(ref, ref, sem).wait()

    def to_group(step, src, dst, sem_send, sem_recv):
        half, block = row_block(step)
        klass, slot = place(half)
        for d in range(1, 8):
            peer = device_of(half, lax.rem(klass + d, 8), slot)
            send(src.at[d, rows_of(block)], dst.at[d, rows_of(block)], sem_send, sem_recv.at[step], peer)

    def stage_weight(step, _):
        half, block = row_block(step)
        klass, slot = place(half)
        flat_ref[...] = jnp.broadcast_to(row_keep[0:1, lanes_of(block)], (TILE, TILE)).T

        def part(r, _):
            at = pl.ds(pl.multiple_of(block * TILE + r * 32, 32), 32)
            flat = flat_ref[pl.ds(pl.multiple_of(r * 32, 32), 32), :]
            tiles = []
            for c in range(8):
                keep = flat * col_keep[0:1, c * TILE : (c + 1) * TILE]
                tiles.append(
                    (variance[at, c * TILE : (c + 1) * TILE].astype(F32) * keep).astype(BF16)
                )
            for d, tile in enumerate(turned(tiles, klass - start + 32)):
                w_send[d, at, :] = tile
            return 0

        lax.fori_loop(0, 4, part, 0)
        to_group(step, w_send, w_recv, send_sem.at[0], w_sem)
        return 0

    lax.fori_loop(0, NCHUNK, stage_weight, 0)
    build_taps(cols_ref, rows_ref, coeff_ref, col_mat, row_mat)
    load_picture.wait()
    column_pass(picture, col_mat, mid)

    def stage_matched(step, _):
        half, block = row_block(step)
        klass, slot = place(half)
        window = mid[pl.ds(block * 8, 10)].reshape(KROWS, IMG)
        matched[...] = jnp.dot(row_mat[...], window, preferred_element_type=F32).astype(BF16)

        def part(r, _):
            at = pl.ds(pl.multiple_of(block * TILE + r * 32, 32), 32)
            inner = pl.ds(pl.multiple_of(r * 32, 32), 32)
            tiles = [matched[inner, c * TILE : (c + 1) * TILE] for c in range(8)]
            for d, tile in enumerate(turned(tiles, klass - start + 32)):
                m_send[d, at, :] = tile
            return 0

        lax.fori_loop(0, 4, part, 0)
        to_group(step, m_send, m_recv, send_sem.at[1], m_sem)
        return 0

    lax.fori_loop(0, NCHUNK, stage_matched, 0)

    def column_slot(exposure, klass):
        begin = sky_ref[exposure, band, 0]
        c = jnp.bitwise_and(klass - begin + 32, 7)
        return lax.shift_right_logical(jnp.bitwise_and(begin + c, 31), 3)

    def reduce_group(step, _):
        half, block = row_block(step)
        klass, slot = place(half)
        wait_for(w_recv.at[pl.ds(1, 7), rows_of(block)], w_sem.at[step])
        wait_for(m_recv.at[pl.ds(1, 7), rows_of(block)], m_sem.at[step])
        rel = []
        for d in range(8):
            source = device_of(half, lax.rem(klass - d + 8, 8), slot)
            rel.append(jnp.full((32, TILE), jnp.bitwise_and(column_slot(source, klass) - slot + 4, 3), jnp.int32))

        def part(r, _):
            at = pl.ds(pl.multiple_of(block * TILE + r * 32, 32), 32)
            inner = pl.ds(pl.multiple_of(r * 32, 32), 32)
            numer = [jnp.zeros((32, TILE), F32) for _ in range(4)]
            denom = [jnp.zeros((32, TILE), F32) for _ in range(4)]
            for d in range(8):
                w = (w_recv if d else w_send)[d, at, :].astype(F32)
                wm = w * (m_recv if d else m_send)[d, at, :].astype(F32)
                for t in range(4):
                    hit = rel[d] == t
                    numer[t] = numer[t] + jnp.where(hit, wm, 0.0)
                    denom[t] = denom[t] + jnp.where(hit, w, 0.0)
            numer_own[at, :] = numer[0]
            denom_own[at, :] = denom[0]
            for t in range(1, 4):
                p_send[t, block, 0, inner, :] = numer[t].astype(BF16)
                p_send[t, block, 1, inner, :] = denom[t].astype(BF16)
            return 0

        lax.fori_loop(0, 4, part, 0)
        for t in range(1, 4):
            peer = device_of(half, klass, lax.rem(slot + t, 4))
            send(p_send.at[t, block], p_recv.at[t, block], send_sem.at[2], p_sem.at[step], peer)
        return 0

    lax.fori_loop(0, NCHUNK, reduce_group, 0)

    def make_template(step, _):
        half, block = row_block(step)
        klass, slot = place(half)
        wait_for(p_recv.at[pl.ds(1, 3), block], p_sem.at[step])
        numer = numer_own[rows_of(block), :]
        denom = denom_own[rows_of(block), :]
        for t in range(1, 4):
            numer = numer + p_recv[t, block, 0].astype(F32)
            denom = denom + p_recv[t, block, 1].astype(F32)
        t_all[0, rows_of(block), :] = (numer / jnp.maximum(denom, 1.0)).astype(BF16)
        for t in range(1, 4):
            peer = device_of(half, klass, lax.rem(slot + t, 4))
            send(t_all.at[0, rows_of(block)], t_all.at[t, rows_of(block)], send_sem.at[3], t_sem.at[step], peer)
        return 0

    lax.fori_loop(0, NCHUNK, make_template, 0)

    def pick_templates(step, _):
        half, block = row_block(step)
        klass, slot = place(half)
        wait_for(t_all.at[pl.ds(1, 3), rows_of(block)], t_sem.at[step])
        for d in range(8):
            target = device_of(half, lax.rem(klass + d, 8), slot)
            rel = jnp.full((TILE, TILE), jnp.bitwise_and(slot - column_slot(target, klass) + 4, 3), jnp.int32)
            value = t_all[0, rows_of(block), :]
            for t in range(1, 4):
                value = jnp.where(rel == t, t_all[t, rows_of(block), :], value)
            q_send[d, rows_of(block), :] = value
        to_group(step, q_send, q_recv, send_sem.at[4], q_sem)
        return 0

    lax.fori_loop(0, NCHUNK, pick_templates, 0)
    save_template = pltpu.make_async_copy(t_all.at[0], template_out, load_sem.at[2])
    save_template.start()

    def subtract(step, _):
        half, block = row_block(step)
        klass, slot = place(half)
        wait_for(q_recv.at[pl.ds(1, 7), rows_of(block)], q_sem.at[step])

        def part(r, _):
            at = pl.ds(pl.multiple_of(block * TILE + r * 32, 32), 32)
            tiles = []
            for i in range(8):
                d = (8 - i) % 8
                m = m_send[i, at, :].astype(F32)
                q = (q_recv if d else q_send)[d, at, :].astype(F32)
                tiles.append((m - q).astype(BF16))
            for c, tile in enumerate(turned(tiles, start - klass + 32)):
                d_out[at, c * TILE : (c + 1) * TILE] = tile
            return 0

        lax.fori_loop(0, 4, part, 0)
        pltpu.make_async_copy(d_out.at[rows_of(block)], difference_out.at[rows_of(block)], out_sem).start()
        return 0

    lax.fori_loop(0, NCHUNK, subtract, 0)
    save_template.wait()
    wait_for(d_out, out_sem)
    wait_for(w_send.at[pl.ds(1, 7)], send_sem.at[0])
    wait_for(m_send.at[pl.ds(1, 7)], send_sem.at[1])
    wait_for(p_send.at[pl.ds(1, 3)], send_sem.at[2])
    wait_for(t_all.at[pl.ds(1, 3)], send_sem.at[3])
    wait_for(q_send.at[pl.ds(1, 7)], send_sem.at[4])


def coadd(picture, variance, planes, sky_columns, basis_rows, basis_cols, coeffs):
    vmem = pl.BlockSpec(memory_space=pltpu.VMEM)
    smem = pl.BlockSpec(memory_space=pltpu.SMEM)
    anyw = pl.BlockSpec(memory_space=pl.ANY)
    tiles = pltpu.VMEM((8, IMG, TILE), BF16)
    parts = pltpu.VMEM((4, NCHUNK, 2, TILE, TILE), BF16)
    return pl.pallas_call(
        coadd_kernel,
        out_shape=(
            jax.ShapeDtypeStruct((IMG, IMG), BF16),
            jax.ShapeDtypeStruct((IMG, TILE), BF16),
        ),
        in_specs=[anyw, anyw, smem, smem, vmem, vmem, smem],
        out_specs=(anyw, anyw),
        scratch_shapes=[
            pltpu.VMEM((IMG, IMG), BF16),
            pltpu.VMEM((IMG, IMG), BF16),
            pltpu.VMEM((8, IMG), F32),
            pltpu.VMEM((8, IMG), F32),
            pltpu.VMEM((2 * TILE, NB * TILE), BF16),
            pltpu.VMEM((TILE, KROWS), BF16),
            pltpu.VMEM((66, NB, 16, IMG), BF16),
            pltpu.VMEM((TILE, IMG), BF16),
            tiles,
            tiles,
            tiles,
            tiles,
            parts,
            parts,
            pltpu.VMEM((IMG, TILE), F32),
            pltpu.VMEM((IMG, TILE), F32),
            pltpu.VMEM((4, IMG, TILE), BF16),
            tiles,
            tiles,
            pltpu.VMEM((TILE, TILE), F32),
            pltpu.VMEM((IMG, IMG), BF16),
            pltpu.SemaphoreType.DMA((3,)),
            pltpu.SemaphoreType.DMA,
            pltpu.SemaphoreType.DMA((5,)),
            pltpu.SemaphoreType.DMA((NCHUNK,)),
            pltpu.SemaphoreType.DMA((NCHUNK,)),
            pltpu.SemaphoreType.DMA((NCHUNK,)),
            pltpu.SemaphoreType.DMA((NCHUNK,)),
            pltpu.SemaphoreType.DMA((NCHUNK,)),
        ],
        compiler_params=pltpu.CompilerParams(
            collective_id=0, has_side_effects=True, vmem_limit_bytes=60 << 20
        ),
        name="coadd",
    )(picture, variance, planes, sky_columns, basis_rows, basis_cols, coeffs)


def with_halo(block, sides, width):
    for axis, dim in sides:
        count = lax.axis_size(axis)
        forward = [(i, (i + 1) % count) for i in range(count)]
        backward = [(target, source) for source, target in forward]
        low = lax.ppermute(
            lax.slice_in_dim(block, block.shape[dim] - width, None, axis=dim), axis, forward
        )
        high = lax.ppermute(lax.slice_in_dim(block, 0, width, axis=dim), axis, backward)
        block = jnp.concatenate([low, block, high], axis=dim)
    return block


def band_matrix(tap_rows, window_width):
    offsets = (
        jnp.arange(window_width, dtype=jnp.int32)[:, None]
        - jnp.arange(TILE, dtype=jnp.int32)[None, :]
    )
    selector = (
        offsets[:, :, None] == jnp.arange(tap_rows.shape[1], dtype=jnp.int32)[None, None, :]
    ).astype(F32)
    return jnp.einsum(
        "wtl,kl->kwt", selector, tap_rows.astype(F32), precision=lax.Precision.HIGHEST
    ).astype(BF16)


def detect(template, detect_taps):
    swap = [(8 * y + 2 * z + c, 8 * z + 2 * y + c) for y in range(4) for z in range(4) for c in range(2)]
    lower = lax.ppermute(template[512:], "sky", swap)
    template = jnp.concatenate([template[:512], lower], 0)
    margin = DTAPS // 2
    width_full = TILE + 2 * margin
    filter_band = band_matrix(detect_taps.astype(BF16), width_full)[0]
    widened = with_halo(template, (("sky", 1),), margin)
    smoothed = jnp.dot(widened, filter_band, preferred_element_type=F32).astype(BF16)
    smooth_padded = jnp.pad(smoothed, ((margin, margin), (0, 0)))
    smooth_blocks = jnp.stack(
        [smooth_padded[TILE * i : TILE * i + width_full] for i in range(8)], 0
    )
    filtered = jnp.einsum(
        "iwx,wt->itx", smooth_blocks, filter_band, preferred_element_type=F32
    ).reshape(IMG, TILE)
    power = filtered * filtered
    pieces = power.reshape(4, IMG // 4, TILE)
    arrived = lax.all_to_all(pieces, "band", split_axis=0, concat_axis=0, tiled=True)
    return arrived.sum(axis=0)


def body(
    exposures,
    inv_variance,
    mask_planes,
    sky_columns,
    basis_rows,
    basis_cols,
    match_coeffs,
    detect_taps,
):
    difference, template = coadd(
        exposures[0, 0],
        inv_variance[0, 0],
        mask_planes[0, 0],
        sky_columns,
        basis_rows,
        basis_cols,
        match_coeffs[0],
    )
    return (difference[None, None], detect(template, detect_taps))


def solution(mesh):
    in_specs = (
        P("sky", "band", None, None),
        P("sky", "band", None, None),
        P("sky", "band", None, None),
        P(),
        P(),
        P(),
        P("sky", "band", None),
        P("band", None),
    )
    out_specs = (P("sky", "band", None, None), P("band", "sky"))
    return jax.shard_map(body, mesh=mesh, in_specs=in_specs, out_specs=out_specs, check_vma=False)
```

time: 447 us -> 103 us (0.23)
  blocking collectives: 120 us -> 0 us
  local copies, waits for them, and re-layouts: 123 us -> 3.93 us
  waiting for transfers between devices: 84.1 us -> 19.6 us
  Pallas kernels: 0 us -> 61.2 us
  other arithmetic: 61.9 us -> 1.16 us
  matrix products: 23.3 us -> 2.01 us
  between operations: 14.3 us -> 0.73 us
    all_to_all x1 -> x0, blocking collectives: 120 us -> none  [body(): lax.all_to_all(send_weight, 'sky', split_axis=1, concat_axis=1, tiled=True)]
    pallas_call x0 -> x1, Pallas kernels: none -> 61.2 us  [coadd(): pl.pallas_call(coadd_kernel, out_shape=(jax.ShapeDtypeStruct((IMG, IMG),...]
    all_to_all x2 -> x1, waiting for transfers between devices: 49.3 us -> 8.08 us  [detect(): lax.all_to_all(pieces, 'band', split_axis=0, concat_axis=0, tiled=True)]
    eq x2 -> x0, other arithmetic: 34.9 us -> none  [keep_pixels(): return jnp.logical_and(row_bits[:, None] == 0, column_bits[None, :] == 0)]
    all_gather x1 -> x0, waiting for transfers between devices: 33.8 us -> none  [subtract_template(): lax.all_gather(template, 'sky', axis=1, tiled=True)]
    unnamed x43 -> x13, local copies, waits for them, and re-layouts: 33.6 us -> 2.92 us
    convert_element_type x3 -> x0, local copies, waits for them, and re-layouts: 29.3 us -> none  [the longest x1 24.6 us: psf_match(): column_pass.reshape(NB, side_length, side_length).astype(jnp.bfloat16)]
    dot_general x7 -> x3, matrix products: 23.3 us -> 2.01 us  [the longest x1 1.05 us: detect(): jnp.einsum('iwx,wt->itx', smooth_blocks, filter_band, preferred_element_t...]
  transfers between devices with their start and end apart: 5 -> 4, of which waited for: 4 -> 3; matrix products, arithmetic and copies ran while one was open for 16% -> 1% of each run, Pallas kernels for 0% -> 0%
where the time goes in v1:
time: 103 us; the launch traced here: 102 us
  Pallas kernels  61.2 us (59%)
  waiting for transfers between devices  19.6 us (19%)
  starting transfers between devices  13.5 us (13%)
  local copies, waits for them, and re-layouts  3.93 us (4%)
  matrix products  2.01 us (2%)
  other arithmetic  1.16 us (1%)
    pallas_call x1, Pallas kernels, coadd(): pl.pallas_call(coadd_kernel, out_shape=(jax.ShapeDtypeStruct((IMG, IMG),...  61.2 us
    all_to_all x1, waiting for transfers between devices, detect(): lax.all_to_all(pieces, 'band', split_axis=0, concat_axis=0, tiled=True)  8.08 us
    ppermute x1, waiting for transfers between devices, detect(): lower = lax.ppermute(template[512:], 'sky', swap)  8.01 us
    ppermute x1, starting transfers between devices, detect(): lower = lax.ppermute(template[512:], 'sky', swap)  5.27 us
    all_to_all x1, starting transfers between devices, detect(): lax.all_to_all(pieces, 'band', split_axis=0, concat_axis=0, tiled=True)  4.29 us
    ppermute x1, starting transfers between devices, with_halo(): lax.ppermute(lax.slice_in_dim(block, 0, width, axis=dim), axis, backward)  3.84 us
    ppermute x1, waiting for transfers between devices, with_halo(): lax.ppermute(lax.slice_in_dim(block, block.shape[dim] - width, None, axis...  3.51 us
    unnamed x13, local copies, waits for them, and re-layouts  2.92 us
  transfers between devices with their start and end apart: 4, of which 3 were waited for; matrix products, arithmetic and copies ran while one was open for 1% of the time, Pallas kernels for 0%

profile of v1, /device:TPU:24, one launch (start us, length us, event | category | flops | bytes accessed | tf_op | source)
XLA Modules:
  0.0 102.1 jit_solution(15838570637450002392)
XLA Ops:
  0.6 1.4 %copy.11.sky_ref = s32[32,4,8]{2,1,0:T(4,128)} copy(s32[32,4,8]{0,2,1:T(8,128)} %param.11) | data formatting | bytes 8192 | tf_op args[3]
  2.1 61.2 %coadd.1 = (bf16[1024,1024]{1,0:T(8,128)(2,1)}, bf16[1024,128]{1,0:T(8,128)(2,1)}) custom-call(bf16[1024,1024]{1,0:T(8,128)(2,1)} %bitcast.55, bf16[1024,1024]{1,0:T(8,128)(2,1)} %bitcast.56, s32[2,35]{1,0:T(2,128)} %bitcast.58, s32[32,4,8]{2,1,0:T(4,128)} %copy.11.sky_ref, f32[9,25]{1,0:T(8,128)} %rows_ref.1, f32[9,25]{1,0:T(8,128)} %cols_ref.1, ...), custom_call_target="tpu_custom_call" | custom-call | tf_op jit(solution)/shard_map/coadd/pallas_call | solution.py:364
  63.2 0.0 copy-start.1
  63.2 1.0 fusion.21
  64.2 5.3 %collective-permute-start = (bf16[512,128]{1,0:T(8,128)(2,1)S(1)}, bf16[512,128]{1,0:T(8,128)(2,1)S(1)}, u32[]{:S(2)}, u32[]{:S(2)}) collective-permute-start(bf16[512,128]{1,0:T(8,128)(2,1)S(1)} %get-tuple-element.9), channel_id=1, source_target_pairs={{0,0},{4,4},{8,32},{12,36},{16,64},{20,68},{24,96},{28,100},{32,8}... | collective-permute-start | bytes 393224 | tf_op jit(solution)/shard_map/ppermute | solution.py:438
  69.5 0.3 iota_compare_fusion
  69.9 8.0 %collective-permute-done = bf16[512,128]{1,0:T(8,128)(2,1)S(1)} collective-permute-done((bf16[512,128]{1,0:T(8,128)(2,1)S(1)}, bf16[512,128]{1,0:T(8,128)(2,1)S(1)}, u32[]{:S(2)}, u32[]{:S(2)}) %collective-permute-start) | collective-permute-done | bytes 131104 | tf_op jit(solution)/shard_map/ppermute | solution.py:438
  77.9 0.1 slice_maximum_fusion
  78.0 0.1 collective-permute-start.1
  78.1 3.8 %collective-permute-start.2 = (bf16[1024,15]{1,0:T(8,128)(2,1)S(1)}, bf16[1024,15]{1,0:T(8,128)(2,1)S(1)}, u32[]{:S(2)}, u32[]{:S(2)}) collective-permute-start(bf16[1024,15]{1,0:T(8,128)(2,1)S(1)} %get-tuple-element.7), channel_id=1, source_target_pairs={{4,0},{8,4},{12,8},{16,12},{20,16},{24,20},{28,24},{32,28},{36,32}... | collective-permute-start | bytes 92168 | tf_op jit(solution)/shard_map/ppermute | solution.py:418
  81.9 0.0 copy-done.1
  81.9 0.5 fusion
  82.5 3.5 %collective-permute-done.1 = bf16[1024,15]{1,0:T(8,128)(2,1)S(1)} collective-permute-done((bf16[1024,15]{1,0:T(8,128)(2,1)S(1)}, bf16[1024,15]{1,0:T(8,128)(2,1)S(1)}, u32[]{:S(2)}, u32[]{:S(2)}) %collective-permute-start.1) | collective-permute-done | bytes 30752 | tf_op jit(solution)/shard_map/ppermute | solution.py:415
  86.0 0.0 collective-permute-done.2
  86.0 0.4 convolution_convert_fusion
  86.4 0.0 copy-start
  86.6 1.1 %convolution_multiply_fusion = f32[128,8,128]{2,0,1:T(8,128)} fusion(bf16[8,158,128]{2,1,0:T(8,128)(2,1)S(1)} %fusion.12, bf16[1,158,128]{2,0,1:T(2,128)(2,1)S(1)} %fusion), kind=kOutput, calls=%fused_computation.3 | convolution fusion | flops 41549824 | bytes 888320 | tf_op jit(solution)/shard_map/iwx,wt->itx/dot_general | solution.py:449
  87.7 4.3 %all-to-all-start = ((f32[4,256,128]{2,1,0:T(8,128)}), f32[4,256,128]{2,1,0:T(8,128)S(1)}, u32[]{:S(2)}, u32[]{:S(2)}) async-start(f32[4,256,128]{2,1,0:T(8,128)} %bitcast.18), calls=%async_computation | async-start | bytes 1048576 | tf_op jit(solution)/shard_map/all_to_all | solution.py:454
  92.0 8.1 %all-to-all-done = f32[4,256,128]{2,1,0:T(8,128)S(1)} async-done(((f32[4,256,128]{2,1,0:T(8,128)}), f32[4,256,128]{2,1,0:T(8,128)S(1)}, u32[]{:S(2)}, u32[]{:S(2)}) %all-to-all-start) | async-done | bytes 524320 | tf_op jit(solution)/shard_map/all_to_all | solution.py:454
  100.1 0.7 reduce_sum.9
  100.7 0.0 copy-done
  100.7 1.3 %copy.29 = bf16[1,1,1024,1024]{3,2,1,0:T(8,128)(2,1)} copy(bf16[1,1,1024,1024]{3,2,1,0:T(8,128)(2,1)S(1)} %bitcast.57) | data formatting | bytes 4194304
  (9 shorter events, 0.2 us)
Async XLA Ops:
  63.2 18.7 %copy-start.1 = (f32[1,31]{1,0:T(1,128)S(1)}, f32[1,31]{1,0:T(1,128)}, u32[]{:S(2)}) copy-start(f32[1,31]{1,0:T(1,128)} %param.15) | copy-start | bytes 376
  64.2 13.6 %collective-permute-start = (bf16[512,128]{1,0:T(8,128)(2,1)S(1)}, bf16[512,128]{1,0:T(8,128)(2,1)S(1)}, u32[]{:S(2)}, u32[]{:S(2)}) collective-permute-start(bf16[512,128]{1,0:T(8,128)(2,1)S(1)} %get-tuple-element.9), channel_id=1, source_target_pairs={{0,0},{4,4},{8,32},{12,36},{16,64},{20,68},{24,96},{28,100},{32,8}... | collective-permute-start | bytes 393224 | tf_op jit(solution)/shard_map/ppermute | solution.py:438
  78.0 8.0 %collective-permute-start.1 = (bf16[1024,15]{1,0:T(8,128)(2,1)S(1)}, bf16[1024,15]{1,0:T(8,128)(2,1)S(1)}, u32[]{:S(2)}, u32[]{:S(2)}) collective-permute-start(bf16[1024,15]{1,0:T(8,128)(2,1)S(1)} %get-tuple-element.6), channel_id=1, source_target_pairs={{0,4},{4,8},{8,12},{12,16},{16,20},{20,24},{24,28},{28,32},{32,36}... | collective-permute-start | bytes 92168 | tf_op jit(solution)/shard_map/ppermute | solution.py:415
  78.1 7.9 %collective-permute-start.2 = (bf16[1024,15]{1,0:T(8,128)(2,1)S(1)}, bf16[1024,15]{1,0:T(8,128)(2,1)S(1)}, u32[]{:S(2)}, u32[]{:S(2)}) collective-permute-start(bf16[1024,15]{1,0:T(8,128)(2,1)S(1)} %get-tuple-element.7), channel_id=1, source_target_pairs={{4,0},{8,4},{12,8},{16,12},{20,16},{24,20},{28,24},{32,28},{36,32}... | collective-permute-start | bytes 92168 | tf_op jit(solution)/shard_map/ppermute | solution.py:418
  86.4 14.3 %copy-start = (bf16[1024,1024]{1,0:T(8,128)(2,1)S(1)}, bf16[1024,1024]{1,0:T(8,128)(2,1)}, u32[]{:S(2)}) copy-start(bf16[1024,1024]{1,0:T(8,128)(2,1)} %get-tuple-element.4) | copy-start | bytes 6291460
  87.7 12.4 %all-to-all-start = ((f32[4,256,128]{2,1,0:T(8,128)}), f32[4,256,128]{2,1,0:T(8,128)S(1)}, u32[]{:S(2)}, u32[]{:S(2)}) async-start(f32[4,256,128]{2,1,0:T(8,128)} %bitcast.18), calls=%async_computation | async-start | bytes 1048576 | tf_op jit(solution)/shard_map/all_to_all | solution.py:454

commit v2 on v1

--- a/solution.py
+++ b/solution.py
@@ -23,6 +23,10 @@
     return pl.ds(pl.multiple_of(block * TILE, TILE), TILE)
 
 
+def quarter_of(block):
+    return pl.ds(pl.multiple_of(block * 256, 256), 256)
+
+
 def lanes_of(block):
     return pl.ds(pl.multiple_of(block * TILE, TILE), TILE)
 
@@ -40,6 +44,11 @@
     klass = jnp.where(half == 0, rest, 2 * y + core)
     slot = jnp.where(half == 0, y, z)
     return klass, slot
+
+
+def turned_column(column):
+    y, rest = lax.div(column, 8), lax.rem(column, 8)
+    return 8 * lax.div(rest, 2) + 2 * y + lax.rem(rest, 2)
 
 
 def row_block(step):
@@ -122,6 +131,31 @@
     lax.fori_loop(0, 8, one, 0)
 
 
+def build_detection(detect_ref, pack_mat, smooth_mat, filter_mat):
+    row = lax.broadcasted_iota(jnp.int32, (IMG, 2 * TILE), 0)
+    lane = lax.broadcasted_iota(jnp.int32, (IMG, 2 * TILE), 1)
+    block, inner = lax.div(row, TILE), lax.rem(row, TILE)
+    last = jnp.logical_and(inner >= 112, lane == block * 16 + inner - 112)
+    first = jnp.logical_and(inner < 16, lane == TILE + block * 16 + inner)
+    pack_mat[...] = jnp.where(jnp.logical_or(last, first), 1.0, 0.0).astype(BF16)
+    taps = detect_ref[...].astype(BF16).astype(F32)
+    taps = jnp.concatenate(
+        [taps, jnp.zeros((1, TILE - DTAPS), F32), jnp.zeros((1, TILE), F32)], 1
+    )
+
+    def ring(shift):
+        base = jnp.broadcast_to(pltpu.roll(taps, shift, 1), (TILE, 2 * TILE))
+        return pltpu.roll(base, 0, 1, stride=1, stride_axis=0)
+
+    table = ring(2 * TILE - 15)
+    table = jnp.concatenate([table[:, :TILE].T, table[:, TILE:].T], 0).astype(BF16)
+    smooth_mat[0:TILE] = table[0:TILE]
+    for b in range(8):
+        smooth_mat[TILE + 16 * b : TILE + 16 * b + 16] = table[240:256]
+        smooth_mat[2 * TILE + 16 * b : 2 * TILE + 16 * b + 16] = table[128:144]
+    filter_mat[...] = ring(1)[:, :160].astype(BF16)
+
+
 def coadd_kernel(
     picture_in,
     variance_in,
@@ -130,8 +164,9 @@
     rows_ref,
     cols_ref,
     coeff_ref,
+    detect_ref,
     difference_out,
-    template_out,
+    detection_out,
     picture,
     variance,
     col_keep,
@@ -153,6 +188,16 @@
     q_recv,
     flat_ref,
     d_out,
+    pack_mat,
+    smooth_mat,
+    filter_mat,
+    natural,
+    e_send,
+    e_recv,
+    smooth,
+    power,
+    b_recv,
+    detection,
     load_sem,
     out_sem,
     send_sem,
@@ -161,6 +206,9 @@
     p_sem,
     t_sem,
     q_sem,
+    x_sem,
+    e_sem,
+    b_sem,
 ):
     own = lax.axis_index("sky")
     band = lax.axis_index("band")
@@ -170,6 +218,23 @@
         for d in range(1, 8):
             peer = device_of(half, lax.rem(klass + d, 8), slot)
             pl.semaphore_signal(barrier, inc=1, device_id=(peer, band), device_id_type=MESH)
+    mirror = turned_column(own)
+    for step in (1, 31):
+        for peer in (
+            lax.rem(own + step, 32),
+            lax.rem(mirror + step, 32),
+            turned_column(lax.rem(own + step, 32)),
+        ):
+            pl.semaphore_signal(barrier, inc=1, device_id=(peer, band), device_id_type=MESH)
+    for step in range(1, 4):
+        pl.semaphore_signal(
+            barrier, inc=1, device_id=(own, lax.rem(band + step, 4)), device_id_type=MESH
+        )
+
+    @pl.when(mirror != own)
+    def _():
+        pl.semaphore_signal(barrier, inc=1, device_id=(mirror, band), device_id_type=MESH)
+
     load_variance = pltpu.make_async_copy(variance_in, variance, load_sem.at[0])
     load_picture = pltpu.make_async_copy(picture_in, picture, load_sem.at[1])
     load_variance.start()
@@ -178,15 +243,15 @@
     col_keep[...] = bit_lanes(planes_ref, 0)
     row_keep[...] = bit_lanes(planes_ref, 1)
     load_variance.wait()
-    pl.semaphore_wait(barrier, 14)
-
-    def send(src, dst, sem_send, sem_recv, device):
+    pl.semaphore_wait(barrier, jnp.where(mirror != own, 24, 23))
+
+    def send(src, dst, sem_send, sem_recv, device, to_band=None):
         pltpu.make_async_remote_copy(
             src_ref=src,
             dst_ref=dst,
             send_sem=sem_send,
             recv_sem=sem_recv,
-            device_id=(device, band),
+            device_id=(device, band if to_band is None else to_band),
             device_id_type=MESH,
         ).start()
 
@@ -224,6 +289,7 @@
 
     lax.fori_loop(0, NCHUNK, stage_weight, 0)
     build_taps(cols_ref, rows_ref, coeff_ref, col_mat, row_mat)
+    build_detection(detect_ref, pack_mat, smooth_mat, filter_mat)
     load_picture.wait()
     column_pass(picture, col_mat, mid)
 
@@ -305,6 +371,26 @@
         return 0
 
     lax.fori_loop(0, NCHUNK, make_template, 0)
+    lower = t_all.at[0, pl.ds(512, 512)]
+
+    @pl.when(mirror != own)
+    def _():
+        send(lower, natural, send_sem.at[5], x_sem, mirror)
+
+    @pl.when(mirror == own)
+    def _():
+        pltpu.make_async_copy(lower, natural, x_sem).start()
+
+    for half in range(2):
+        column = mirror if half else own
+        wide = jnp.concatenate(
+            [t_all[0, half * 512 + 64 * b : half * 512 + 64 * b + 64, :] for b in range(8)], 1
+        )
+        packed = jnp.dot(wide, pack_mat[...], preferred_element_type=F32).astype(BF16)
+        for side in range(2):
+            e_send[half, side] = packed[:, side * TILE : (side + 1) * TILE]
+            peer = lax.rem(column + (31 if side else 1), 32)
+            send(e_send.at[half, side], e_recv.at[half, side], send_sem.at[6], e_sem, peer)
 
     def pick_templates(step, _):
         half, block = row_block(step)
@@ -321,8 +407,30 @@
         return 0
 
     lax.fori_loop(0, NCHUNK, pick_templates, 0)
-    save_template = pltpu.make_async_copy(t_all.at[0], template_out, load_sem.at[2])
-    save_template.start()
+    wait_for(natural, x_sem)
+    wait_for(e_recv, e_sem)
+    smooth[0:16] = jnp.zeros((16, TILE), BF16)
+    smooth[IMG + 16 : IMG + 32] = jnp.zeros((16, TILE), BF16)
+    group = lax.div(lax.broadcasted_iota(jnp.int32, (64, TILE), 1), 16)
+    for quarter in range(4):
+        half = quarter // 2
+        pieces = []
+        for b in range(4 * (quarter % 2), 4 * (quarter % 2) + 4):
+            here = natural[64 * b : 64 * b + 64, :] if half else t_all[0, 64 * b : 64 * b + 64, :]
+            zero = jnp.zeros((64, TILE), BF16)
+            left = jnp.where(group == b, e_recv[half, 0], zero)
+            right = jnp.where(group == b, e_recv[half, 1], zero)
+            pieces.append(jnp.concatenate([here, left, right], 1))
+        got = jnp.dot(jnp.concatenate(pieces, 0), smooth_mat[...], preferred_element_type=F32)
+        smooth[16 + 256 * quarter : 272 + 256 * quarter] = got.astype(BF16)
+    for i in range(8):
+        got = jnp.dot(
+            filter_mat[...], smooth[TILE * i : TILE * i + 160], preferred_element_type=F32
+        )
+        power[TILE * i : TILE * i + TILE] = got * got
+    for t in range(1, 4):
+        target = lax.rem(band + t, 4)
+        send(power.at[quarter_of(target)], b_recv.at[t - 1], send_sem.at[7], b_sem, own, target)
 
     def subtract(step, _):
         half, block = row_block(step)
@@ -346,7 +454,11 @@
         return 0
 
     lax.fori_loop(0, NCHUNK, subtract, 0)
-    save_template.wait()
+    wait_for(b_recv, b_sem)
+    detection[...] = power[quarter_of(band), :] + b_recv[0] + b_recv[1] + b_recv[2]
+    save = pltpu.make_async_copy(detection, detection_out, load_sem.at[2])
+    save.start()
+    save.wait()
     wait_for(d_out, out_sem)
     wait_for(w_send.at[pl.ds(1, 7)], send_sem.at[0])
     wait_for(m_send.at[pl.ds(1, 7)], send_sem.at[1])
@@ -354,8 +466,15 @@
     wait_for(t_all.at[pl.ds(1, 3)], send_sem.at[3])
     wait_for(q_send.at[pl.ds(1, 7)], send_sem.at[4])
 
-
-def coadd(picture, variance, planes, sky_columns, basis_rows, basis_cols, coeffs):
+    @pl.when(mirror != own)
+    def _():
+        wait_for(natural, send_sem.at[5])
+
+    wait_for(e_send, send_sem.at[6])
+    wait_for(b_recv, send_sem.at[7])
+
+
+def coadd(picture, variance, planes, sky_columns, basis_rows, basis_cols, coeffs, detect_taps):
     vmem = pl.BlockSpec(memory_space=pltpu.VMEM)
     smem = pl.BlockSpec(memory_space=pltpu.SMEM)
     anyw = pl.BlockSpec(memory_space=pl.ANY)
@@ -365,9 +484,9 @@
         coadd_kernel,
         out_shape=(
             jax.ShapeDtypeStruct((IMG, IMG), BF16),
-            jax.ShapeDtypeStruct((IMG, TILE), BF16),
+            jax.ShapeDtypeStruct((IMG // 4, TILE), F32),
         ),
-        in_specs=[anyw, anyw, smem, smem, vmem, vmem, smem],
+        in_specs=[anyw, anyw, smem, smem, vmem, vmem, smem, vmem],
         out_specs=(anyw, anyw),
         scratch_shapes=[
             pltpu.VMEM((IMG, IMG), BF16),
@@ -391,68 +510,33 @@
             tiles,
             pltpu.VMEM((TILE, TILE), F32),
             pltpu.VMEM((IMG, IMG), BF16),
+            pltpu.VMEM((IMG, 2 * TILE), BF16),
+            pltpu.VMEM((3 * TILE, TILE), BF16),
+            pltpu.VMEM((TILE, 160), BF16),
+            pltpu.VMEM((512, TILE), BF16),
+            pltpu.VMEM((2, 2, 64, TILE), BF16),
+            pltpu.VMEM((2, 2, 64, TILE), BF16),
+            pltpu.VMEM((IMG + 32, TILE), BF16),
+            pltpu.VMEM((IMG, TILE), F32),
+            pltpu.VMEM((3, IMG // 4, TILE), F32),
+            pltpu.VMEM((IMG // 4, TILE), F32),
             pltpu.SemaphoreType.DMA((3,)),
             pltpu.SemaphoreType.DMA,
-            pltpu.SemaphoreType.DMA((5,)),
+            pltpu.SemaphoreType.DMA((8,)),
             pltpu.SemaphoreType.DMA((NCHUNK,)),
             pltpu.SemaphoreType.DMA((NCHUNK,)),
             pltpu.SemaphoreType.DMA((NCHUNK,)),
             pltpu.SemaphoreType.DMA((NCHUNK,)),
             pltpu.SemaphoreType.DMA((NCHUNK,)),
+            pltpu.SemaphoreType.DMA,
+            pltpu.SemaphoreType.DMA,
+            pltpu.SemaphoreType.DMA,
         ],
         compiler_params=pltpu.CompilerParams(
             collective_id=0, has_side_effects=True, vmem_limit_bytes=60 << 20
         ),
         name="coadd",
-    )(picture, variance, planes, sky_columns, basis_rows, basis_cols, coeffs)
-
-
-def with_halo(block, sides, width):
-    for axis, dim in sides:
-        count = lax.axis_size(axis)
-        forward = [(i, (i + 1) % count) for i in range(count)]
-        backward = [(target, source) for source, target in forward]
-        low = lax.ppermute(
-            lax.slice_in_dim(block, block.shape[dim] - width, None, axis=dim), axis, forward
-        )
-        high = lax.ppermute(lax.slice_in_dim(block, 0, width, axis=dim), axis, backward)
-        block = jnp.concatenate([low, block, high], axis=dim)
-    return block
-
-
-def band_matrix(tap_rows, window_width):
-    offsets = (
-        jnp.arange(window_width, dtype=jnp.int32)[:, None]
-        - jnp.arange(TILE, dtype=jnp.int32)[None, :]
-    )
-    selector = (
-        offsets[:, :, None] == jnp.arange(tap_rows.shape[1], dtype=jnp.int32)[None, None, :]
-    ).astype(F32)
-    return jnp.einsum(
-        "wtl,kl->kwt", selector, tap_rows.astype(F32), precision=lax.Precision.HIGHEST
-    ).astype(BF16)
-
-
-def detect(template, detect_taps):
-    swap = [(8 * y + 2 * z + c, 8 * z + 2 * y + c) for y in range(4) for z in range(4) for c in range(2)]
-    lower = lax.ppermute(template[512:], "sky", swap)
-    template = jnp.concatenate([template[:512], lower], 0)
-    margin = DTAPS // 2
-    width_full = TILE + 2 * margin
-    filter_band = band_matrix(detect_taps.astype(BF16), width_full)[0]
-    widened = with_halo(template, (("sky", 1),), margin)
-    smoothed = jnp.dot(widened, filter_band, preferred_element_type=F32).astype(BF16)
-    smooth_padded = jnp.pad(smoothed, ((margin, margin), (0, 0)))
-    smooth_blocks = jnp.stack(
-        [smooth_padded[TILE * i : TILE * i + width_full] for i in range(8)], 0
-    )
-    filtered = jnp.einsum(
-        "iwx,wt->itx", smooth_blocks, filter_band, preferred_element_type=F32
-    ).reshape(IMG, TILE)
-    power = filtered * filtered
-    pieces = power.reshape(4, IMG // 4, TILE)
-    arrived = lax.all_to_all(pieces, "band", split_axis=0, concat_axis=0, tiled=True)
-    return arrived.sum(axis=0)
+    )(picture, variance, planes, sky_columns, basis_rows, basis_cols, coeffs, detect_taps)
 
 
 def body(
@@ -465,7 +549,7 @@
     match_coeffs,
     detect_taps,
 ):
-    difference, template = coadd(
+    difference, detection = coadd(
         exposures[0, 0],
         inv_variance[0, 0],
         mask_planes[0, 0],
@@ -473,8 +557,9 @@
         basis_rows,
         basis_cols,
         match_coeffs[0],
+        detect_taps,
     )
-    return (difference[None, None], detect(template, detect_taps))
+    return (difference[None, None], detection)
 
 
 def solution(mesh):

time: 103 us -> 79.1 us (0.77)
  waiting for transfers between devices: 19.6 us -> 0 us
  starting transfers between devices: 13.5 us -> 0 us
  Pallas kernels: 61.2 us -> 73 us
  matrix products: 2.01 us -> 0 us
  local copies, waits for them, and re-layouts: 3.93 us -> 5.2 us
  other arithmetic: 1.16 us -> 0 us
    pallas_call x1, Pallas kernels: 61.2 us -> 73 us  [coadd(): pl.pallas_call(coadd_kernel, out_shape=(jax.ShapeDtypeStruct((IMG, IMG),...]
    ppermute x3 -> x0, waiting for transfers between devices: 11.5 us -> none  [the longest x1 8.01 us: detect(): lower = lax.ppermute(template[512:], 'sky', swap)]
    ppermute x3 -> x0, starting transfers between devices: 9.19 us -> none  [the longest x1 5.27 us: detect(): lower = lax.ppermute(template[512:], 'sky', swap)]
    all_to_all x1 -> x0, waiting for transfers between devices: 8.08 us -> none  [detect(): lax.all_to_all(pieces, 'band', split_axis=0, concat_axis=0, tiled=True)]
    all_to_all x1 -> x0, starting transfers between devices: 4.29 us -> none  [detect(): lax.all_to_all(pieces, 'band', split_axis=0, concat_axis=0, tiled=True)]
    unnamed x13 -> x5, local copies, waits for them, and re-layouts: 2.92 us -> 5.2 us
    dot_general x3 -> x0, matrix products: 2.01 us -> none  [the longest x1 1.05 us: detect(): jnp.einsum('iwx,wt->itx', smooth_blocks, filter_band, preferred_element_t...]
  transfers between devices with their start and end apart: 4 -> 0, of which waited for: 3 -> 0; matrix products, arithmetic and copies ran while one was open for 1% -> 0% of each run, Pallas kernels for 0% -> 0%
where the time goes in v2:
time: 79.1 us; the launch traced here: 78.9 us
  Pallas kernels  73 us (92%)
  local copies, waits for them, and re-layouts  5.2 us (7%)
    pallas_call x1, Pallas kernels, coadd(): pl.pallas_call(coadd_kernel, out_shape=(jax.ShapeDtypeStruct((IMG, IMG),...  73 us
    unnamed x5, local copies, waits for them, and re-layouts  5.2 us

profile of v2, /device:TPU:24, one launch (start us, length us, event | category | flops | bytes accessed | tf_op | source)
XLA Modules:
  0.0 78.9 jit_solution(4916617886206439572)
XLA Ops:
  0.6 1.4 %copy.10.sky_ref = s32[32,4,8]{2,1,0:T(4,128)} copy(s32[32,4,8]{0,2,1:T(8,128)} %param.11) | data formatting | bytes 8192 | tf_op args[3]
  2.1 73.0 %coadd.1 = (bf16[1024,1024]{1,0:T(8,128)(2,1)}, f32[256,128]{1,0:T(8,128)}) custom-call(bf16[1024,1024]{1,0:T(8,128)(2,1)} %bitcast.6, bf16[1024,1024]{1,0:T(8,128)(2,1)} %bitcast.7, s32[2,35]{1,0:T(2,128)} %bitcast.8, s32[32,4,8]{2,1,0:T(4,128)} %copy.10.sky_ref, f32[9,25]{1,0:T(8,128)} %rows_ref.1, f32[9,25]{1,0:T(8,128)} %cols_ref.1, f32[1,9]{1,0:T(1,128)} %bitcast.9, ...), custom_call_target="tpu_custom_call" | custom-call | tf_op jit(solution)/shard_map/coadd/pallas_call | solution.py:483
  75.1 0.0 copy-start
  75.1 3.1 %copy.13 = bf16[1,1,1024,1024]{3,2,1,0:T(8,128)(2,1)} copy(bf16[1,1,1024,1024]{3,2,1,0:T(8,128)(2,1)} %bitcast.5) | data formatting | bytes 4194304
  78.2 0.0 copy-done
  78.2 0.7 copy.14
Async XLA Ops:
  75.1 3.1 %copy-start = (f32[256,128]{1,0:T(8,128)S(1)}, f32[256,128]{1,0:T(8,128)}, u32[]{:S(2)}) copy-start(f32[256,128]{1,0:T(8,128)} %get-tuple-element.9) | copy-start | bytes 393220

commit v3 on v2

v3 whole, which is shorter than its diff:
```python
import jax
import jax.numpy as jnp
from jax import lax
from jax.experimental import pallas as pl
from jax.experimental.pallas import tpu as pltpu
from jax.sharding import PartitionSpec as P

TILE = 128
NB = 9
TAPS = 25
DTAPS = 31
IMG = 1024
HALO = 12
STRIP = NB * 16
KROWS = 10 * STRIP
CHUNK = 128
STEPS = 512 // CHUNK
MESH = pl.DeviceIdType.MESH
F32 = jnp.float32
BF16 = jnp.bfloat16


def rows_of(block):
    return pl.ds(pl.multiple_of(block * TILE, TILE), TILE)


def quarter_of(block):
    return pl.ds(pl.multiple_of(block * 256, 256), 256)


def lanes_of(block):
    return pl.ds(pl.multiple_of(block * TILE, TILE), TILE)


def device_of(half, klass, slot):
    if half == 0:
        return 8 * slot + klass
    return 8 * lax.div(klass, 2) + 2 * slot + lax.rem(klass, 2)


def place(half):
    own = lax.axis_index("sky")
    y, rest = lax.div(own, 8), lax.rem(own, 8)
    z, core = lax.div(rest, 2), lax.rem(rest, 2)
    return (2 * y + core, z) if half else (rest, y)


def turned_column(column):
    y, rest = lax.div(column, 8), lax.rem(column, 8)
    return 8 * lax.div(rest, 2) + 2 * y + lax.rem(rest, 2)


def chunk_of(half, step):
    return pl.ds(pl.multiple_of(half * 512 + step * CHUNK, CHUNK), CHUNK)


def strip_of(half, step, part):
    return pl.ds(pl.multiple_of(half * 512 + step * CHUNK + part * 32, 32), 32)


def turned(tiles, amount):
    for bit in (1, 2, 4):
        take = jnp.bitwise_and(jnp.full(tiles[0].shape, amount, jnp.int32), bit) != 0
        tiles = [jnp.where(take, tiles[(i + bit) % 8], tiles[i]) for i in range(8)]
    return tiles


def bit_lanes(planes_ref, plane):
    lane = lax.broadcasted_iota(jnp.int32, (8, IMG), 1)
    word = jnp.zeros((8, IMG), jnp.int32)
    first = jnp.zeros((8, IMG), jnp.int32)
    for index in range(35):
        inside = lane >= 30 * index
        word = jnp.where(inside, planes_ref[plane, index], word)
        first = jnp.where(inside, 30 * index, first)
    bit = jnp.bitwise_and(lax.shift_right_logical(word, lane - first), 1)
    return (1 - bit).astype(F32)


def build_taps(cols_ref, rows_ref, coeff_ref, col_mat, row_mat):
    pad = jnp.zeros((1, TILE - TAPS), F32)
    far = jnp.zeros((1, TILE), F32)
    for k in range(NB):
        taps = (cols_ref[k : k + 1, :] * coeff_ref[0, k]).astype(BF16).astype(F32)
        base = pltpu.roll(jnp.concatenate([taps, pad, far], 1), 2 * TILE - HALO, 1)
        ring = pltpu.roll(jnp.broadcast_to(base, (TILE, 2 * TILE)), 0, 1, stride=1, stride_axis=0)
        col_mat[:, k * TILE : (k + 1) * TILE] = ring.T.astype(BF16)
    place_w = lax.broadcasted_iota(jnp.int32, (TILE, 512), 0)
    place_l = lax.broadcasted_iota(jnp.int32, (TILE, 512), 1)
    picker = jnp.where(
        jnp.logical_and(place_l == lax.div(place_w, 16) * STRIP + lax.rem(place_w, 16), place_w < 48),
        1.0,
        0.0,
    ).astype(BF16)
    stacked = []
    for k in range(NB):
        taps = rows_ref[k : k + 1, :].astype(BF16).astype(F32)
        base = pltpu.roll(jnp.concatenate([taps, pad], 1), 4, 1)
        stacked.append(pltpu.roll(jnp.broadcast_to(base, (16, TILE)), 0, 1, stride=1, stride_axis=0))
    spread = jnp.dot(
        jnp.concatenate(stacked, 0).astype(BF16), picker, preferred_element_type=F32
    )
    first = jnp.zeros((16, 512), F32)
    for k in range(NB):
        first = first + pltpu.roll(spread[16 * k : 16 * k + 16], 16 * k, 1)
    first = jnp.concatenate([first, jnp.zeros((16, 1024), F32)], 1)
    for u in range(8):
        row_mat[16 * u : 16 * u + 16, :] = pltpu.roll(first, STRIP * u, 1)[:, :KROWS].astype(BF16)


def column_pass(picture, col_mat, mid):
    mid[0] = jnp.zeros((NB, 16, IMG), BF16)
    mid[65] = jnp.zeros((NB, 16, IMG), BF16)
    near = lax.broadcasted_iota(jnp.int32, (IMG, TILE), 1) < 64

    def one(j, _):
        here = picture[:, lanes_of(j)]
        after = picture[:, lanes_of(jnp.minimum(j + 1, 7))]
        before = picture[:, lanes_of(jnp.maximum(j - 1, 0))]
        zero = jnp.zeros_like(here)
        after = jnp.where(jnp.broadcast_to(j < 7, near.shape), after, zero)
        before = jnp.where(jnp.broadcast_to(j > 0, near.shape), before, zero)
        lhs = jnp.concatenate([here, jnp.where(near, after, before)], 1)
        for k in range(0, NB, 2):
            count = min(2, NB - k)
            got = jnp.dot(
                lhs, col_mat[:, k * TILE : (k + count) * TILE], preferred_element_type=F32
            ).astype(BF16)
            for t in range(count):
                mid[1:65, k + t, :, lanes_of(j)] = got[:, t * TILE : (t + 1) * TILE].reshape(64, 16, TILE)
        return 0

    lax.fori_loop(0, 8, one, 0)


def build_detection(detect_ref, pack_mat, smooth_mat, filter_mat):
    row = lax.broadcasted_iota(jnp.int32, (IMG, 2 * TILE), 0)
    lane = lax.broadcasted_iota(jnp.int32, (IMG, 2 * TILE), 1)
    block, inner = lax.div(row, TILE), lax.rem(row, TILE)
    last = jnp.logical_and(inner >= 112, lane == block * 16 + inner - 112)
    first = jnp.logical_and(inner < 16, lane == TILE + block * 16 + inner)
    pack_mat[...] = jnp.where(jnp.logical_or(last, first), 1.0, 0.0).astype(BF16)
    taps = detect_ref[...].astype(BF16).astype(F32)
    taps = jnp.concatenate(
        [taps, jnp.zeros((1, TILE - DTAPS), F32), jnp.zeros((1, TILE), F32)], 1
    )

    def ring(shift):
        base = jnp.broadcast_to(pltpu.roll(taps, shift, 1), (TILE, 2 * TILE))
        return pltpu.roll(base, 0, 1, stride=1, stride_axis=0)

    table = ring(2 * TILE - 15)
    table = jnp.concatenate([table[:, :TILE].T, table[:, TILE:].T], 0).astype(BF16)
    smooth_mat[0:TILE] = table[0:TILE]
    for b in range(8):
        smooth_mat[TILE + 16 * b : TILE + 16 * b + 16] = table[240:256]
        smooth_mat[2 * TILE + 16 * b : 2 * TILE + 16 * b + 16] = table[128:144]
    filter_mat[...] = ring(1)[:, :160].astype(BF16)


def coadd_kernel(
    picture_in,
    variance_in,
    planes_ref,
    sky_in,
    rows_ref,
    cols_ref,
    coeff_ref,
    detect_ref,
    difference_out,
    detection_out,
    picture,
    variance,
    sky_ref,
    col_keep,
    col_mat,
    row_mat,
    mid,
    matched,
    w_send,
    w_recv,
    m_send,
    m_recv,
    p_send,
    p_recv,
    numer_own,
    denom_own,
    t_all,
    q_send,
    q_recv,
    flat_ref,
    pack_mat,
    smooth_mat,
    filter_mat,
    natural,
    e_send,
    e_recv,
    smooth,
    power,
    b_recv,
    load_sem,
    send_sem,
    w_sem,
    m_sem,
    p_sem,
    t_sem,
    q_sem,
    x_sem,
    e_sem,
    b_sem,
):
    own = lax.axis_index("sky")
    band = lax.axis_index("band")
    barrier = pltpu.get_barrier_semaphore()
    places, group, sources, ring = [], [], [], []
    for half in range(2):
        klass, slot = place(half)
        places.append((klass, slot))
        group.append([device_of(half, lax.rem(klass + d, 8), slot) for d in range(8)])
        sources.append([device_of(half, lax.rem(klass + 8 - d, 8), slot) for d in range(8)])
        ring.append([device_of(half, klass, lax.rem(slot + t, 4)) for t in range(4)])
        for d in range(1, 8):
            pl.semaphore_signal(
                barrier, inc=1, device_id=(group[half][d], band), device_id_type=MESH
            )
    mirror = turned_column(own)
    for step in (1, 31):
        for peer in (
            lax.rem(own + step, 32),
            lax.rem(mirror + step, 32),
            turned_column(lax.rem(own + step, 32)),
        ):
            pl.semaphore_signal(barrier, inc=1, device_id=(peer, band), device_id_type=MESH)
    for step in range(1, 4):
        pl.semaphore_signal(
            barrier, inc=1, device_id=(own, lax.rem(band + step, 4)), device_id_type=MESH
        )

    @pl.when(mirror != own)
    def _():
        pl.semaphore_signal(barrier, inc=1, device_id=(mirror, band), device_id_type=MESH)

    load_sky = pltpu.make_async_copy(sky_in, sky_ref, load_sem.at[2])
    load_variance = pltpu.make_async_copy(variance_in, variance, load_sem.at[0])
    load_picture = pltpu.make_async_copy(picture_in, picture, load_sem.at[1])
    load_sky.start()
    load_variance.start()
    load_picture.start()
    col_keep[...] = bit_lanes(planes_ref, 0)
    row_keep = bit_lanes(planes_ref, 1)
    for i in range(8):
        flat_ref[i * TILE : (i + 1) * TILE] = jnp.broadcast_to(
            row_keep[0:1, i * TILE : (i + 1) * TILE], (TILE, TILE)
        ).T
    load_sky.wait()
    start = sky_ref[band, 0, own]
    turn = [places[half][0] - start + 32 for half in range(2)]
    load_variance.wait()
    pl.semaphore_wait(barrier, jnp.where(mirror != own, 24, 23))

    def send(src, dst, sem_send, sem_recv, device, to_band=None):
        pltpu.make_async_remote_copy(
            src_ref=src,
            dst_ref=dst,
            send_sem=sem_send,
            recv_sem=sem_recv,
            device_id=(device, band if to_band is None else to_band),
            device_id_type=MESH,
        ).start()

    def wait_for(ref, sem):
        pltpu.make_async_copy(ref, ref, sem).wait()

    def to_group(half, step, src, dst, sem_send, sem_recv):
        rows = chunk_of(half, step)
        for d in range(1, 8):
            send(
                src.at[d, rows], dst.at[d, rows], sem_send, sem_recv.at[half, step], group[half][d]
            )

    def stage_weight(step, _):
        for half in range(2):

            def part(r, _):
                at = strip_of(half, step, r)
                flat = flat_ref[at, :]
                tiles = []
                for c in range(8):
                    keep = flat * col_keep[0:1, c * TILE : (c + 1) * TILE]
                    tiles.append(
                        (variance[at, c * TILE : (c + 1) * TILE].astype(F32) * keep).astype(BF16)
                    )
                for d, tile in enumerate(turned(tiles, turn[half])):
                    w_send[d, at, :] = tile
                return 0

            lax.fori_loop(0, CHUNK // 32, part, 0)
            to_group(half, step, w_send, w_recv, send_sem.at[0], w_sem)
        return 0

    lax.fori_loop(0, STEPS, stage_weight, 0)
    build_taps(cols_ref, rows_ref, coeff_ref, col_mat, row_mat)
    build_detection(detect_ref, pack_mat, smooth_mat, filter_mat)
    load_picture.wait()
    column_pass(picture, col_mat, mid)

    def stage_matched(step, _):
        for half in range(2):

            def block(i, _):
                first = half * 32 + step * (CHUNK // 16) + i * 8
                window = mid[pl.ds(first, 10)].reshape(KROWS, IMG)
                matched[...] = jnp.dot(
                    row_mat[...], window, preferred_element_type=F32
                ).astype(BF16)

                def part(r, _):
                    at = strip_of(half, step, i * 4 + r)
                    inner = pl.ds(pl.multiple_of(r * 32, 32), 32)
                    tiles = [matched[inner, c * TILE : (c + 1) * TILE] for c in range(8)]
                    for d, tile in enumerate(turned(tiles, turn[half])):
                        m_send[d, at, :] = tile
                    return 0

                lax.fori_loop(0, 4, part, 0)
                return 0

            lax.fori_loop(0, CHUNK // TILE, block, 0)
            to_group(half, step, m_send, m_recv, send_sem.at[1], m_sem)
        return 0

    lax.fori_loop(0, STEPS, stage_matched, 0)

    def column_slot(exposure, klass):
        begin = sky_ref[band, 0, exposure]
        c = jnp.bitwise_and(klass - begin + 32, 7)
        return lax.shift_right_logical(jnp.bitwise_and(begin + c, 31), 3)

    def reduce_group(step, _):
        for half in range(2):
            klass, slot = places[half]
            rows = chunk_of(half, step)
            piece = half * STEPS + step
            wait_for(w_recv.at[pl.ds(1, 7), rows], w_sem.at[half, step])
            wait_for(m_recv.at[pl.ds(1, 7), rows], m_sem.at[half, step])
            rel = [
                jnp.full(
                    (32, TILE),
                    jnp.bitwise_and(column_slot(sources[half][d], klass) - slot + 4, 3),
                    jnp.int32,
                )
                for d in range(8)
            ]

            def part(r, _):
                at = strip_of(half, step, r)
                inner = pl.ds(pl.multiple_of(r * 32, 32), 32)
                numer = [jnp.zeros((32, TILE), F32) for _ in range(4)]
                denom = [jnp.zeros((32, TILE), F32) for _ in range(4)]
                for d in range(8):
                    w = (w_recv if d else w_send)[d, at, :].astype(F32)
                    wm = w * (m_recv if d else m_send)[d, at, :].astype(F32)
                    for t in range(4):
                        hit = rel[d] == t
                        numer[t] = numer[t] + jnp.where(hit, wm, 0.0)
                        denom[t] = denom[t] + jnp.where(hit, w, 0.0)
                numer_own[at, :] = numer[0]
                denom_own[at, :] = denom[0]
                for t in range(1, 4):
                    p_send[t, piece, 0, inner, :] = numer[t].astype(BF16)
                    p_send[t, piece, 1, inner, :] = denom[t].astype(BF16)
                return 0

            lax.fori_loop(0, CHUNK // 32, part, 0)
            for t in range(1, 4):
                send(
                    p_send.at[t, piece],
                    p_recv.at[t, piece],
                    send_sem.at[2],
                    p_sem.at[half, step],
                    ring[half][t],
                )
        return 0

    lax.fori_loop(0, STEPS, reduce_group, 0)

    def make_template(step, _):
        for half in range(2):
            rows = chunk_of(half, step)
            piece = half * STEPS + step
            wait_for(p_recv.at[pl.ds(1, 3), piece], p_sem.at[half, step])

            def part(r, _):
                at = strip_of(half, step, r)
                inner = pl.ds(pl.multiple_of(r * 32, 32), 32)
                numer = numer_own[at, :]
                denom = denom_own[at, :]
                for t in range(1, 4):
                    numer = numer + p_recv[t, piece, 0, inner, :].astype(F32)
                    denom = denom + p_recv[t, piece, 1, inner, :].astype(F32)
                t_all[0, at, :] = (numer / jnp.maximum(denom, 1.0)).astype(BF16)
                return 0

            lax.fori_loop(0, CHUNK // 32, part, 0)
            for t in range(1, 4):
                send(
                    t_all.at[0, rows],
                    t_all.at[t, rows],
                    send_sem.at[3],
                    t_sem.at[half, step],
                    ring[half][t],
                )
        return 0

    lax.fori_loop(0, STEPS, make_template, 0)
    lower = t_all.at[0, pl.ds(512, 512)]

    @pl.when(mirror != own)
    def _():
        send(lower, natural, send_sem.at[5], x_sem, mirror)

    @pl.when(mirror == own)
    def _():
        pltpu.make_async_copy(lower, natural, x_sem).start()

    for half in range(2):
        column = mirror if half else own
        wide = jnp.concatenate(
            [t_all[0, half * 512 + 64 * b : half * 512 + 64 * b + 64, :] for b in range(8)], 1
        )
        packed = jnp.dot(wide, pack_mat[...], preferred_element_type=F32).astype(BF16)
        for side in range(2):
            e_send[half, side] = packed[:, side * TILE : (side + 1) * TILE]
            peer = lax.rem(column + (31 if side else 1), 32)
            send(e_send.at[half, side], e_recv.at[half, side], send_sem.at[6], e_sem, peer)

    def pick_templates(step, _):
        for half in range(2):
            klass, slot = places[half]
            rows = chunk_of(half, step)
            wait_for(t_all.at[pl.ds(1, 3), rows], t_sem.at[half, step])
            rel = [
                jnp.full(
                    (32, TILE),
                    jnp.bitwise_and(slot - column_slot(group[half][d], klass) + 4, 3),
                    jnp.int32,
                )
                for d in range(8)
            ]

            def part(r, _):
                at = strip_of(half, step, r)
                values = [t_all[t, at, :] for t in range(4)]
                for d in range(8):
                    value = values[0]
                    for t in range(1, 4):
                        value = jnp.where(rel[d] == t, values[t], value)
                    q_send[d, at, :] = value
                return 0

            lax.fori_loop(0, CHUNK // 32, part, 0)
            to_group(half, step, q_send, q_recv, send_sem.at[4], q_sem)
        return 0

    lax.fori_loop(0, STEPS, pick_templates, 0)
    wait_for(natural, x_sem)
    wait_for(e_recv, e_sem)
    smooth[0:16] = jnp.zeros((16, TILE), BF16)
    smooth[IMG + 16 : IMG + 32] = jnp.zeros((16, TILE), BF16)
    lane_group = lax.div(lax.broadcasted_iota(jnp.int32, (64, TILE), 1), 16)
    for quarter in range(4):
        half = quarter // 2
        pieces = []
        for b in range(4 * (quarter % 2), 4 * (quarter % 2) + 4):
            here = natural[64 * b : 64 * b + 64, :] if half else t_all[0, 64 * b : 64 * b + 64, :]
            zero = jnp.zeros((64, TILE), BF16)
            left = jnp.where(lane_group == b, e_recv[half, 0], zero)
            right = jnp.where(lane_group == b, e_recv[half, 1], zero)
            pieces.append(jnp.concatenate([here, left, right], 1))
        got = jnp.dot(jnp.concatenate(pieces, 0), smooth_mat[...], preferred_element_type=F32)
        smooth[16 + 256 * quarter : 272 + 256 * quarter] = got.astype(BF16)
    for i in range(8):
        got = jnp.dot(
            filter_mat[...], smooth[TILE * i : TILE * i + 160], preferred_element_type=F32
        )
        power[TILE * i : TILE * i + TILE] = got * got
    for t in range(1, 4):
        target = lax.rem(band + t, 4)
        send(power.at[quarter_of(target)], b_recv.at[t - 1], send_sem.at[7], b_sem, own, target)

    def subtract(step, _):
        for half in range(2):
            wait_for(q_recv.at[pl.ds(1, 7), chunk_of(half, step)], q_sem.at[half, step])

            def part(r, _):
                at = strip_of(half, step, r)
                tiles = []
                for i in range(8):
                    d = (8 - i) % 8
                    m = m_send[i, at, :].astype(F32)
                    q = (q_recv if d else q_send)[d, at, :].astype(F32)
                    tiles.append((m - q).astype(BF16))
                for c, tile in enumerate(turned(tiles, 64 - turn[half])):
                    difference_out[at, c * TILE : (c + 1) * TILE] = tile
                return 0

            lax.fori_loop(0, CHUNK // 32, part, 0)
        return 0

    lax.fori_loop(0, STEPS, subtract, 0)
    wait_for(b_recv, b_sem)
    detection_out[...] = power[quarter_of(band), :] + b_recv[0] + b_recv[1] + b_recv[2]
    wait_for(w_send.at[pl.ds(1, 7)], send_sem.at[0])
    wait_for(m_send.at[pl.ds(1, 7)], send_sem.at[1])
    wait_for(p_send.at[pl.ds(1, 3)], send_sem.at[2])
    wait_for(t_all.at[pl.ds(1, 3)], send_sem.at[3])
    wait_for(q_send.at[pl.ds(1, 7)], send_sem.at[4])

    @pl.when(mirror != own)
    def _():
        wait_for(natural, send_sem.at[5])

    wait_for(e_send, send_sem.at[6])
    wait_for(b_recv, send_sem.at[7])


def coadd(picture, variance, planes, sky_columns, basis_rows, basis_cols, coeffs, detect_taps):
    vmem = pl.BlockSpec(memory_space=pltpu.VMEM)
    smem = pl.BlockSpec(memory_space=pltpu.SMEM)
    anyw = pl.BlockSpec(memory_space=pl.ANY)
    tiles = pltpu.VMEM((8, IMG, TILE), BF16)
    parts = pltpu.VMEM((4, 2 * STEPS, 2, CHUNK, TILE), BF16)
    arrivals = pltpu.SemaphoreType.DMA((2, STEPS))
    return pl.pallas_call(
        coadd_kernel,
        out_shape=(pltpu.VMEM((IMG, IMG), BF16), pltpu.VMEM((IMG // 4, TILE), F32)),
        in_specs=[anyw, anyw, smem, anyw, vmem, vmem, smem, vmem],
        out_specs=(vmem, vmem),
        scratch_shapes=[
            pltpu.VMEM((IMG, IMG), BF16),
            pltpu.VMEM((IMG, IMG), BF16),
            pltpu.SMEM((4, 8, 32), jnp.int32),
            pltpu.VMEM((8, IMG), F32),
            pltpu.VMEM((2 * TILE, NB * TILE), BF16),
            pltpu.VMEM((TILE, KROWS), BF16),
            pltpu.VMEM((66, NB, 16, IMG), BF16),
            pltpu.VMEM((TILE, IMG), BF16),
            tiles,
            tiles,
            tiles,
            tiles,
            parts,
            parts,
            pltpu.VMEM((IMG, TILE), F32),
            pltpu.VMEM((IMG, TILE), F32),
            pltpu.VMEM((4, IMG, TILE), BF16),
            tiles,
            tiles,
            pltpu.VMEM((IMG, TILE), F32),
            pltpu.VMEM((IMG, 2 * TILE), BF16),
            pltpu.VMEM((3 * TILE, TILE), BF16),
            pltpu.VMEM((TILE, 160), BF16),
            pltpu.VMEM((512, TILE), BF16),
            pltpu.VMEM((2, 2, 64, TILE), BF16),
            pltpu.VMEM((2, 2, 64, TILE), BF16),
            pltpu.VMEM((IMG + 32, TILE), BF16),
            pltpu.VMEM((IMG, TILE), F32),
            pltpu.VMEM((3, IMG // 4, TILE), F32),
            pltpu.SemaphoreType.DMA((3,)),
            pltpu.SemaphoreType.DMA((8,)),
            arrivals,
            arrivals,
            arrivals,
            arrivals,
            arrivals,
            pltpu.SemaphoreType.DMA,
            pltpu.SemaphoreType.DMA,
            pltpu.SemaphoreType.DMA,
        ],
        compiler_params=pltpu.CompilerParams(
            collective_id=0, has_side_effects=True, vmem_limit_bytes=54 << 20
        ),
        name="coadd",
    )(picture, variance, planes, sky_columns, basis_rows, basis_cols, coeffs, detect_taps)


def body(
    exposures,
    inv_variance,
    mask_planes,
    sky_columns,
    basis_rows,
    basis_cols,
    match_coeffs,
    detect_taps,
):
    difference, detection = coadd(
        exposures[0, 0],
        inv_variance[0, 0],
        mask_planes[0, 0],
        jnp.transpose(sky_columns, (1, 2, 0)),
        basis_rows,
        basis_cols,
        match_coeffs[0],
        detect_taps,
    )
    return (difference[None, None], detection)


def solution(mesh):
    in_specs = (
        P("sky", "band", None, None),
        P("sky", "band", None, None),
        P("sky", "band", None, None),
        P(),
        P(),
        P(),
        P("sky", "band", None),
        P("band", None),
    )
    out_specs = (P("sky", "band", None, None), P("band", "sky"))
    return jax.shard_map(body, mesh=mesh, in_specs=in_specs, out_specs=out_specs, check_vma=False)
```

time: 79.1 us -> 72.9 us (0.922)
  local copies, waits for them, and re-layouts: 5.2 us -> 1.98 us
  Pallas kernels: 73 us -> 70.1 us
    unnamed x5 -> x2, local copies, waits for them, and re-layouts: 5.2 us -> 1.98 us
    pallas_call x1, Pallas kernels: 73 us -> 70.1 us  [coadd(): pl.pallas_call(coadd_kernel, out_shape=(pltpu.VMEM((IMG, IMG), BF16), plt...]
where the time goes in v3:
time: 72.9 us; the launch traced here: 72.7 us
  Pallas kernels  70.1 us (96%)
  local copies, waits for them, and re-layouts  1.98 us (3%)
    pallas_call x1, Pallas kernels, coadd(): pl.pallas_call(coadd_kernel, out_shape=(pltpu.VMEM((IMG, IMG), BF16), plt...  70.1 us
    unnamed x2, local copies, waits for them, and re-layouts  1.98 us

profile of v3, /device:TPU:24, one launch (start us, length us, event | category | flops | bytes accessed | tf_op | source)
XLA Modules:
  0.0 72.7 jit_solution(15421184886808056621)
XLA Ops:
  0.6 70.1 %coadd.1 = (bf16[1024,1024]{1,0:T(8,128)(2,1)S(1)}, f32[256,128]{1,0:T(8,128)S(1)}) custom-call(bf16[1024,1024]{1,0:T(8,128)(2,1)} %bitcast.7, bf16[1024,1024]{1,0:T(8,128)(2,1)} %bitcast.8, s32[2,35]{1,0:T(2,128)} %bitcast.10, s32[4,8,32]{2,1,0:T(8,128)} %bitcast.9, f32[9,25]{1,0:T(8,128)} %rows_ref.1, f32[9,25]{1,0:T(8,128)} %cols_ref.1, f32[1,9]{1,0:T(1,128)} %bitcast.11, ...), custom_call_target="tpu_custom_call" | custom-call | tf_op jit(solution)/shard_map/coadd/pallas_call | solution.py:534
  70.8 1.3 %copy.12 = bf16[1,1,1024,1024]{3,2,1,0:T(8,128)(2,1)} copy(bf16[1,1,1024,1024]{3,2,1,0:T(8,128)(2,1)S(1)} %bitcast.6) | data formatting | bytes 4194304
  72.1 0.7 copy.13

commit v4 on v3

--- a/solution.py
+++ b/solution.py
@@ -15,6 +15,8 @@
 KROWS = 10 * STRIP
 CHUNK = 128
 STEPS = 512 // CHUNK
+HALF = CHUNK // 2
+AHEAD = 2
 MESH = pl.DeviceIdType.MESH
 F32 = jnp.float32
 BF16 = jnp.bfloat16
@@ -52,6 +54,10 @@
 
 def chunk_of(half, step):
     return pl.ds(pl.multiple_of(half * 512 + step * CHUNK, CHUNK), CHUNK)
+
+
+def half_chunk_of(half, step, low):
+    return pl.ds(pl.multiple_of(half * 512 + step * CHUNK + low * HALF, HALF), HALF)
 
 
 def strip_of(half, step, part):
@@ -183,6 +189,7 @@
     m_recv,
     p_send,
     p_recv,
+    o_recv,
     numer_own,
     denom_own,
     t_all,
@@ -197,13 +204,16 @@
     e_recv,
     smooth,
     power,
+    power_out,
     b_recv,
     load_sem,
     send_sem,
     w_sem,
     m_sem,
     p_sem,
+    o_sem,
     t_sem,
+    f_sem,
     q_sem,
     x_sem,
     e_sem,
@@ -236,9 +246,12 @@
             barrier, inc=1, device_id=(own, lax.rem(band + step, 4)), device_id_type=MESH
         )
 
-    @pl.when(mirror != own)
-    def _():
-        pl.semaphore_signal(barrier, inc=1, device_id=(mirror, band), device_id_type=MESH)
+    for z in range(4):
+        holder = 8 * places[1][1] + 2 * z + lax.rem(own, 2)
+
+        @pl.when(holder != own)
+        def _():
+            pl.semaphore_signal(barrier, inc=1, device_id=(holder, band), device_id_type=MESH)
 
     load_sky = pltpu.make_async_copy(sky_in, sky_ref, load_sem.at[2])
     load_variance = pltpu.make_async_copy(variance_in, variance, load_sem.at[0])
@@ -256,7 +269,7 @@
     start = sky_ref[band, 0, own]
     turn = [places[half][0] - start + 32 for half in range(2)]
     load_variance.wait()
-    pl.semaphore_wait(barrier, jnp.where(mirror != own, 24, 23))
+    pl.semaphore_wait(barrier, jnp.where(mirror != own, 27, 26))
 
     def send(src, dst, sem_send, sem_recv, device, to_band=None):
         pltpu.make_async_remote_copy(
@@ -329,7 +342,6 @@
             to_group(half, step, m_send, m_recv, send_sem.at[1], m_sem)
         return 0
 
-    lax.fori_loop(0, STEPS, stage_matched, 0)
 
     def column_slot(exposure, klass):
         begin = sky_ref[band, 0, exposure]
@@ -352,93 +364,122 @@
                 for d in range(8)
             ]
 
-            def part(r, _):
-                at = strip_of(half, step, r)
-                inner = pl.ds(pl.multiple_of(r * 32, 32), 32)
-                numer = [jnp.zeros((32, TILE), F32) for _ in range(4)]
-                denom = [jnp.zeros((32, TILE), F32) for _ in range(4)]
-                for d in range(8):
-                    w = (w_recv if d else w_send)[d, at, :].astype(F32)
-                    wm = w * (m_recv if d else m_send)[d, at, :].astype(F32)
-                    for t in range(4):
-                        hit = rel[d] == t
-                        numer[t] = numer[t] + jnp.where(hit, wm, 0.0)
-                        denom[t] = denom[t] + jnp.where(hit, w, 0.0)
-                numer_own[at, :] = numer[0]
-                denom_own[at, :] = denom[0]
-                for t in range(1, 4):
-                    p_send[t, piece, 0, inner, :] = numer[t].astype(BF16)
-                    p_send[t, piece, 1, inner, :] = denom[t].astype(BF16)
-                return 0
-
-            lax.fori_loop(0, CHUNK // 32, part, 0)
-            for t in range(1, 4):
+            for top in range(2):
+
+                def part(r, _):
+                    at = strip_of(half, step, top * (HALF // 32) + r)
+                    inner = pl.ds(pl.multiple_of(r * 32, 32), 32)
+                    numer = [jnp.zeros((32, TILE), F32) for _ in range(4)]
+                    denom = [jnp.zeros((32, TILE), F32) for _ in range(4)]
+                    for d in range(8):
+                        w = (w_recv if d else w_send)[d, at, :].astype(F32)
+                        wm = w * (m_recv if d else m_send)[d, at, :].astype(F32)
+                        for t in range(4):
+                            hit = rel[d] == t
+                            numer[t] = numer[t] + jnp.where(hit, wm, 0.0)
+                            denom[t] = denom[t] + jnp.where(hit, w, 0.0)
+                    numer_own[at, :] = numer[0]
+                    denom_own[at, :] = denom[0]
+                    for t in range(1, 4):
+                        p_send[t, piece, top, 0, inner, :] = numer[t].astype(BF16)
+                        p_send[t, piece, top, 1, inner, :] = denom[t].astype(BF16)
+                    return 0
+
+                lax.fori_loop(0, HALF // 32, part, 0)
+            after, before = ring[half][1], ring[half][3]
+            arrive = p_sem.at[half, step]
+            onward = o_sem.at[half, step]
+            send(p_send.at[2, piece, 0], o_recv.at[0, piece], send_sem.at[2], onward, after)
+            send(p_send.at[2, piece, 1], o_recv.at[1, piece], send_sem.at[2], onward, before)
+            send(p_send.at[1, piece, 1], p_recv.at[0, piece, 1], send_sem.at[2], arrive, after)
+            send(p_send.at[3, piece, 0], p_recv.at[1, piece, 0], send_sem.at[2], arrive, before)
+        return 0
+
+    def combine(step, _):
+        for half in range(2):
+            piece = half * STEPS + step
+            wait_for(o_recv.at[:, piece], o_sem.at[half, step])
+            for side, t, top in ((0, 1, 0), (1, 3, 1)):
+                for kind in range(2):
+                    total = p_send[t, piece, top, kind].astype(F32) + o_recv[
+                        side, piece, kind
+                    ].astype(F32)
+                    p_send[t, piece, top, kind] = total.astype(BF16)
                 send(
-                    p_send.at[t, piece],
-                    p_recv.at[t, piece],
+                    p_send.at[t, piece, top],
+                    p_recv.at[side, piece, top],
                     send_sem.at[2],
                     p_sem.at[half, step],
                     ring[half][t],
                 )
         return 0
 
-    lax.fori_loop(0, STEPS, reduce_group, 0)
-
     def make_template(step, _):
         for half in range(2):
             rows = chunk_of(half, step)
             piece = half * STEPS + step
-            wait_for(p_recv.at[pl.ds(1, 3), piece], p_sem.at[half, step])
-
-            def part(r, _):
-                at = strip_of(half, step, r)
-                inner = pl.ds(pl.multiple_of(r * 32, 32), 32)
-                numer = numer_own[at, :]
-                denom = denom_own[at, :]
-                for t in range(1, 4):
-                    numer = numer + p_recv[t, piece, 0, inner, :].astype(F32)
-                    denom = denom + p_recv[t, piece, 1, inner, :].astype(F32)
-                t_all[0, at, :] = (numer / jnp.maximum(denom, 1.0)).astype(BF16)
-                return 0
-
-            lax.fori_loop(0, CHUNK // 32, part, 0)
-            for t in range(1, 4):
-                send(
-                    t_all.at[0, rows],
-                    t_all.at[t, rows],
-                    send_sem.at[3],
-                    t_sem.at[half, step],
-                    ring[half][t],
-                )
-        return 0
-
-    lax.fori_loop(0, STEPS, make_template, 0)
-    lower = t_all.at[0, pl.ds(512, 512)]
-
-    @pl.when(mirror != own)
-    def _():
-        send(lower, natural, send_sem.at[5], x_sem, mirror)
-
-    @pl.when(mirror == own)
-    def _():
-        pltpu.make_async_copy(lower, natural, x_sem).start()
-
-    for half in range(2):
-        column = mirror if half else own
-        wide = jnp.concatenate(
-            [t_all[0, half * 512 + 64 * b : half * 512 + 64 * b + 64, :] for b in range(8)], 1
-        )
-        packed = jnp.dot(wide, pack_mat[...], preferred_element_type=F32).astype(BF16)
-        for side in range(2):
-            e_send[half, side] = packed[:, side * TILE : (side + 1) * TILE]
-            peer = lax.rem(column + (31 if side else 1), 32)
-            send(e_send.at[half, side], e_recv.at[half, side], send_sem.at[6], e_sem, peer)
+            wait_for(p_recv.at[:, piece], p_sem.at[half, step])
+            for top in range(2):
+
+                def part(r, _):
+                    at = strip_of(half, step, top * (HALF // 32) + r)
+                    inner = pl.ds(pl.multiple_of(r * 32, 32), 32)
+                    numer = numer_own[at, :]
+                    denom = denom_own[at, :]
+                    for side in range(2):
+                        numer = numer + p_recv[side, piece, top, 0, inner, :].astype(F32)
+                        denom = denom + p_recv[side, piece, top, 1, inner, :].astype(F32)
+                    t_all[0, at, :] = (numer / jnp.maximum(denom, 1.0)).astype(BF16)
+                    return 0
+
+                lax.fori_loop(0, HALF // 32, part, 0)
+            arrive = t_sem.at[half, step]
+            send(t_all.at[0, rows], t_all.at[1, rows], send_sem.at[3], arrive, ring[half][1])
+            send(t_all.at[0, rows], t_all.at[2, rows], send_sem.at[3], arrive, ring[half][3])
+        return 0
+
+    def forward(step, _):
+        for half in range(2):
+            wait_for(t_all.at[pl.ds(1, 2), chunk_of(half, step)], t_sem.at[half, step])
+            arrive = f_sem.at[half, step]
+            top, low = half_chunk_of(half, step, 0), half_chunk_of(half, step, 1)
+            send(t_all.at[1, top], t_all.at[3, top], send_sem.at[3], arrive, ring[half][1])
+            send(t_all.at[2, low], t_all.at[3, low], send_sem.at[3], arrive, ring[half][3])
+        return 0
+
+    def send_edges():
+        for half in range(2):
+            column = mirror if half else own
+            wide = jnp.concatenate(
+                [t_all[0, half * 512 + 64 * b : half * 512 + 64 * b + 64, :] for b in range(8)], 1
+            )
+            packed = jnp.dot(wide, pack_mat[...], preferred_element_type=F32).astype(BF16)
+            for side in range(2):
+                e_send[half, side] = packed[:, side * TILE : (side + 1) * TILE]
+                peer = lax.rem(column + (31 if side else 1), 32)
+                send(e_send.at[half, side], e_recv.at[half, side], send_sem.at[6], e_sem, peer)
+
+    def send_home(src, into, target, step):
+        @pl.when(target != own)
+        def _():
+            send(src, into, send_sem.at[5], x_sem.at[step], target)
+
+        @pl.when(target == own)
+        def _():
+            pltpu.make_async_copy(src, into, x_sem.at[step]).start()
 
     def pick_templates(step, _):
-        for half in range(2):
+        for half in (1, 0):
             klass, slot = places[half]
             rows = chunk_of(half, step)
-            wait_for(t_all.at[pl.ds(1, 3), rows], t_sem.at[half, step])
+            wait_for(t_all.at[3, rows], f_sem.at[half, step])
+            if half:
+                strip = strip_of(1, step, slot * (CHUNK // TILE))
+                into = natural.at[strip_of(0, step, slot * (CHUNK // TILE))]
+                for held, t in ((0, 0), (1, 1), (3, 2), (2, 3)):
+                    send_home(
+                        t_all.at[held, strip], into, 8 * lax.rem(slot + 4 - t, 4) + klass, step
+                    )
             rel = [
                 jnp.full(
                     (32, TILE),
@@ -450,7 +491,7 @@
 
             def part(r, _):
                 at = strip_of(half, step, r)
-                values = [t_all[t, at, :] for t in range(4)]
+                values = [t_all[place, at, :] for place in (0, 1, 3, 2)]
                 for d in range(8):
                     value = values[0]
                     for t in range(1, 4):
@@ -462,31 +503,92 @@
             to_group(half, step, q_send, q_recv, send_sem.at[4], q_sem)
         return 0
 
-    lax.fori_loop(0, STEPS, pick_templates, 0)
-    wait_for(natural, x_sem)
-    wait_for(e_recv, e_sem)
+    stages = (
+        (stage_matched, -AHEAD),
+        (reduce_group, 0),
+        (combine, 1),
+        (make_template, 2),
+        (forward, 3),
+        (pick_templates, 4),
+    )
+
+    def tick(n, _):
+        for stage, lag in stages:
+            if lag >= 0:
+
+                @pl.when(jnp.logical_and(n >= lag, n < STEPS + lag))
+                def _():
+                    stage(n - lag, 0)
+
+            else:
+
+                @pl.when(n < STEPS + lag)
+                def _():
+                    stage(n - lag, 0)
+
+            if stage is make_template:
+
+                @pl.when(n == STEPS + 1)
+                def _():
+                    send_edges()
+
+        return 0
+
+    lax.fori_loop(0, AHEAD, stage_matched, 0)
+    lax.fori_loop(0, STEPS + 4, tick, 0)
     smooth[0:16] = jnp.zeros((16, TILE), BF16)
     smooth[IMG + 16 : IMG + 32] = jnp.zeros((16, TILE), BF16)
     lane_group = lax.div(lax.broadcasted_iota(jnp.int32, (64, TILE), 1), 16)
-    for quarter in range(4):
-        half = quarter // 2
+
+    def smooth_rows(i):
+        half = i // 4
         pieces = []
-        for b in range(4 * (quarter % 2), 4 * (quarter % 2) + 4):
-            here = natural[64 * b : 64 * b + 64, :] if half else t_all[0, 64 * b : 64 * b + 64, :]
+        for b in range(2 * (i % 4), 2 * (i % 4) + 2):
+            here = (natural if half else t_all.at[0])[64 * b : 64 * b + 64, :]
             zero = jnp.zeros((64, TILE), BF16)
             left = jnp.where(lane_group == b, e_recv[half, 0], zero)
             right = jnp.where(lane_group == b, e_recv[half, 1], zero)
             pieces.append(jnp.concatenate([here, left, right], 1))
         got = jnp.dot(jnp.concatenate(pieces, 0), smooth_mat[...], preferred_element_type=F32)
-        smooth[16 + 256 * quarter : 272 + 256 * quarter] = got.astype(BF16)
-    for i in range(8):
+        smooth[16 + TILE * i : 16 + TILE * i + TILE] = got.astype(BF16)
+
+    def filter_rows(i):
         got = jnp.dot(
             filter_mat[...], smooth[TILE * i : TILE * i + 160], preferred_element_type=F32
         )
         power[TILE * i : TILE * i + TILE] = got * got
-    for t in range(1, 4):
-        target = lax.rem(band + t, 4)
-        send(power.at[quarter_of(target)], b_recv.at[t - 1], send_sem.at[7], b_sem, own, target)
+        power_out[TILE * i : TILE * i + TILE] = (got * got).astype(BF16)
+
+    def send_power(target):
+        @pl.when(target != band)
+        def _():
+            place_in = lax.rem(band - target + 4, 4) - 1
+            send(
+                power_out.at[pl.ds(256 * target, 256)],
+                b_recv.at[place_in],
+                send_sem.at[7],
+                b_sem,
+                own,
+                target,
+            )
+
+    wait_for(e_recv, e_sem)
+    for i in range(4):
+        smooth_rows(i)
+    wait_for(natural.at[pl.ds(0, CHUNK)], x_sem.at[0])
+    smooth_rows(4)
+    for i in range(4):
+        filter_rows(i)
+    send_power(0)
+    send_power(1)
+    for step in range(1, STEPS):
+        wait_for(natural.at[pl.ds(step * CHUNK, CHUNK)], x_sem.at[step])
+    for i in range(5, 8):
+        smooth_rows(i)
+    for i in range(4, 8):
+        filter_rows(i)
+    send_power(2)
+    send_power(3)
 
     def subtract(step, _):
         for half in range(2):
@@ -509,7 +611,12 @@
 
     lax.fori_loop(0, STEPS, subtract, 0)
     wait_for(b_recv, b_sem)
-    detection_out[...] = power[quarter_of(band), :] + b_recv[0] + b_recv[1] + b_recv[2]
+    detection_out[...] = (
+        power[quarter_of(band), :]
+        + b_recv[0].astype(F32)
+        + b_recv[1].astype(F32)
+        + b_recv[2].astype(F32)
+    )
     wait_for(w_send.at[pl.ds(1, 7)], send_sem.at[0])
     wait_for(m_send.at[pl.ds(1, 7)], send_sem.at[1])
     wait_for(p_send.at[pl.ds(1, 3)], send_sem.at[2])
@@ -520,6 +627,10 @@
     def _():
         wait_for(natural, send_sem.at[5])
 
+    @pl.when(mirror == own)
+    def _():
+        wait_for(natural.at[pl.ds(0, 3 * TILE)], send_sem.at[5])
+
     wait_for(e_send, send_sem.at[6])
     wait_for(b_recv, send_sem.at[7])
 
@@ -529,7 +640,6 @@
     smem = pl.BlockSpec(memory_space=pltpu.SMEM)
     anyw = pl.BlockSpec(memory_space=pl.ANY)
     tiles = pltpu.VMEM((8, IMG, TILE), BF16)
-    parts = pltpu.VMEM((4, 2 * STEPS, 2, CHUNK, TILE), BF16)
     arrivals = pltpu.SemaphoreType.DMA((2, STEPS))
     return pl.pallas_call(
         coadd_kernel,
@@ -549,8 +659,9 @@
             tiles,
             tiles,
             tiles,
-            parts,
-            parts,
+            pltpu.VMEM((4, 2 * STEPS, 2, 2, HALF, TILE), BF16),
+            pltpu.VMEM((2, 2 * STEPS, 2, 2, HALF, TILE), BF16),
+            pltpu.VMEM((2, 2 * STEPS, 2, HALF, TILE), BF16),
             pltpu.VMEM((IMG, TILE), F32),
             pltpu.VMEM((IMG, TILE), F32),
             pltpu.VMEM((4, IMG, TILE), BF16),
@@ -565,7 +676,8 @@
             pltpu.VMEM((2, 2, 64, TILE), BF16),
             pltpu.VMEM((IMG + 32, TILE), BF16),
             pltpu.VMEM((IMG, TILE), F32),
-            pltpu.VMEM((3, IMG // 4, TILE), F32),
+            pltpu.VMEM((IMG, TILE), BF16),
+            pltpu.VMEM((3, IMG // 4, TILE), BF16),
             pltpu.SemaphoreType.DMA((3,)),
             pltpu.SemaphoreType.DMA((8,)),
             arrivals,
@@ -573,7 +685,9 @@
             arrivals,
             arrivals,
             arrivals,
-            pltpu.SemaphoreType.DMA,
+            arrivals,
+            arrivals,
+            pltpu.SemaphoreType.DMA((STEPS,)),
             pltpu.SemaphoreType.DMA,
             pltpu.SemaphoreType.DMA,
         ],

time: 72.9 us -> 69 us (0.947)
  the two profiles are of different devices: /device:TPU:24 before, /device:TPU:6 now
where the time goes in v4:
time: 69 us; the launch traced here: 68.9 us
  Pallas kernels  66.3 us (96%)
  local copies, waits for them, and re-layouts  1.98 us (3%)
    pallas_call x1, Pallas kernels, coadd(): pl.pallas_call(coadd_kernel, out_shape=(pltpu.VMEM((IMG, IMG), BF16), plt...  66.3 us
    unnamed x2, local copies, waits for them, and re-layouts  1.98 us

profile of v4, /device:TPU:6, one launch (start us, length us, event | category | flops | bytes accessed | tf_op | source)
XLA Modules:
  0.0 68.9 jit_solution(4201679485828330505)
XLA Ops:
  0.6 66.3 %coadd.1 = (bf16[1024,1024]{1,0:T(8,128)(2,1)S(1)}, f32[256,128]{1,0:T(8,128)S(1)}) custom-call(bf16[1024,1024]{1,0:T(8,128)(2,1)} %bitcast.7, bf16[1024,1024]{1,0:T(8,128)(2,1)} %bitcast.8, s32[2,35]{1,0:T(2,128)} %bitcast.10, s32[4,8,32]{2,1,0:T(8,128)} %bitcast.9, f32[9,25]{1,0:T(8,128)} %rows_ref.1, f32[9,25]{1,0:T(8,128)} %cols_ref.1, f32[1,9]{1,0:T(1,128)} %bitcast.11, ...), custom_call_target="tpu_custom_call" | custom-call | tf_op jit(solution)/shard_map/coadd/pallas_call | solution.py:644
  66.9 1.3 %copy.12 = bf16[1,1,1024,1024]{3,2,1,0:T(8,128)(2,1)} copy(bf16[1,1,1024,1024]{3,2,1,0:T(8,128)(2,1)S(1)} %bitcast.6) | data formatting | bytes 4194304
  68.2 0.7 copy.13

commit v5 on v4

--- a/solution.py
+++ b/solution.py
@@ -234,24 +234,10 @@
                 barrier, inc=1, device_id=(group[half][d], band), device_id_type=MESH
             )
     mirror = turned_column(own)
-    for step in (1, 31):
-        for peer in (
-            lax.rem(own + step, 32),
-            lax.rem(mirror + step, 32),
-            turned_column(lax.rem(own + step, 32)),
-        ):
-            pl.semaphore_signal(barrier, inc=1, device_id=(peer, band), device_id_type=MESH)
     for step in range(1, 4):
         pl.semaphore_signal(
             barrier, inc=1, device_id=(own, lax.rem(band + step, 4)), device_id_type=MESH
         )
-
-    for z in range(4):
-        holder = 8 * places[1][1] + 2 * z + lax.rem(own, 2)
-
-        @pl.when(holder != own)
-        def _():
-            pl.semaphore_signal(barrier, inc=1, device_id=(holder, band), device_id_type=MESH)
 
     load_sky = pltpu.make_async_copy(sky_in, sky_ref, load_sem.at[2])
     load_variance = pltpu.make_async_copy(variance_in, variance, load_sem.at[0])
@@ -269,7 +255,6 @@
     start = sky_ref[band, 0, own]
     turn = [places[half][0] - start + 32 for half in range(2)]
     load_variance.wait()
-    pl.semaphore_wait(barrier, jnp.where(mirror != own, 27, 26))
 
     def send(src, dst, sem_send, sem_recv, device, to_band=None):
         pltpu.make_async_remote_copy(
@@ -308,10 +293,20 @@
                 return 0
 
             lax.fori_loop(0, CHUNK // 32, part, 0)
-            to_group(half, step, w_send, w_recv, send_sem.at[0], w_sem)
         return 0
 
     lax.fori_loop(0, STEPS, stage_weight, 0)
+    pl.semaphore_wait(barrier, 17)
+    for half in range(2):
+        rows = pl.ds(512 * half, 512)
+        for d in range(1, 8):
+            send(
+                w_send.at[d, rows],
+                w_recv.at[d, rows],
+                send_sem.at[0],
+                w_sem.at[half],
+                group[half][d],
+            )
     build_taps(cols_ref, rows_ref, coeff_ref, col_mat, row_mat)
     build_detection(detect_ref, pack_mat, smooth_mat, filter_mat)
     load_picture.wait()
@@ -349,11 +344,15 @@
         return lax.shift_right_logical(jnp.bitwise_and(begin + c, 31), 3)
 
     def reduce_group(step, _):
-        for half in range(2):
+        for half in (1, 0):
             klass, slot = places[half]
             rows = chunk_of(half, step)
             piece = half * STEPS + step
-            wait_for(w_recv.at[pl.ds(1, 7), rows], w_sem.at[half, step])
+
+            @pl.when(step == 0)
+            def _():
+                wait_for(w_recv.at[pl.ds(1, 7), pl.ds(512 * half, 512)], w_sem.at[half])
+
             wait_for(m_recv.at[pl.ds(1, 7), rows], m_sem.at[half, step])
             rel = [
                 jnp.full(
@@ -396,7 +395,7 @@
         return 0
 
     def combine(step, _):
-        for half in range(2):
+        for half in (1, 0):
             piece = half * STEPS + step
             wait_for(o_recv.at[:, piece], o_sem.at[half, step])
             for side, t, top in ((0, 1, 0), (1, 3, 1)):
@@ -415,7 +414,7 @@
         return 0
 
     def make_template(step, _):
-        for half in range(2):
+        for half in (1, 0):
             rows = chunk_of(half, step)
             piece = half * STEPS + step
             wait_for(p_recv.at[:, piece], p_sem.at[half, step])
@@ -439,7 +438,7 @@
         return 0
 
     def forward(step, _):
-        for half in range(2):
+        for half in (1, 0):
             wait_for(t_all.at[pl.ds(1, 2), chunk_of(half, step)], t_sem.at[half, step])
             arrive = f_sem.at[half, step]
             top, low = half_chunk_of(half, step, 0), half_chunk_of(half, step, 1)
@@ -503,39 +502,25 @@
             to_group(half, step, q_send, q_recv, send_sem.at[4], q_sem)
         return 0
 
-    stages = (
-        (stage_matched, -AHEAD),
-        (reduce_group, 0),
-        (combine, 1),
-        (make_template, 2),
-        (forward, 3),
-        (pick_templates, 4),
-    )
-
-    def tick(n, _):
-        for stage, lag in stages:
-            if lag >= 0:
-
-                @pl.when(jnp.logical_and(n >= lag, n < STEPS + lag))
-                def _():
-                    stage(n - lag, 0)
-
-            else:
-
-                @pl.when(n < STEPS + lag)
-                def _():
-                    stage(n - lag, 0)
-
-            if stage is make_template:
-
-                @pl.when(n == STEPS + 1)
-                def _():
-                    send_edges()
-
-        return 0
-
-    lax.fori_loop(0, AHEAD, stage_matched, 0)
-    lax.fori_loop(0, STEPS + 4, tick, 0)
+    def subtract(step, _):
+        for half in range(2):
+            wait_for(q_recv.at[pl.ds(1, 7), chunk_of(half, step)], q_sem.at[half, step])
+
+            def part(r, _):
+                at = strip_of(half, step, r)
+                tiles = []
+                for i in range(8):
+                    d = (8 - i) % 8
+                    m = m_send[i, at, :].astype(F32)
+                    q = (q_recv if d else q_send)[d, at, :].astype(F32)
+                    tiles.append((m - q).astype(BF16))
+                for c, tile in enumerate(turned(tiles, 64 - turn[half])):
+                    difference_out[at, c * TILE : (c + 1) * TILE] = tile
+                return 0
+
+            lax.fori_loop(0, CHUNK // 32, part, 0)
+        return 0
+
     smooth[0:16] = jnp.zeros((16, TILE), BF16)
     smooth[IMG + 16 : IMG + 32] = jnp.zeros((16, TILE), BF16)
     lane_group = lax.div(lax.broadcasted_iota(jnp.int32, (64, TILE), 1), 16)
@@ -572,15 +557,55 @@
                 target,
             )
 
-    wait_for(e_recv, e_sem)
-    for i in range(4):
-        smooth_rows(i)
-    wait_for(natural.at[pl.ds(0, CHUNK)], x_sem.at[0])
-    smooth_rows(4)
-    for i in range(4):
-        filter_rows(i)
-    send_power(0)
-    send_power(1)
+    def upper_detection():
+        wait_for(e_recv, e_sem)
+        for i in range(4):
+            smooth_rows(i)
+        wait_for(natural.at[pl.ds(0, CHUNK)], x_sem.at[0])
+        smooth_rows(4)
+        for i in range(4):
+            filter_rows(i)
+        send_power(0)
+        send_power(1)
+
+    stages = (
+        (stage_matched, -AHEAD),
+        (reduce_group, 0),
+        (combine, 1),
+        (make_template, 2),
+        (forward, 3),
+        (pick_templates, 4),
+    )
+
+    def tick(n, _):
+        @pl.when(n == STEPS + 3)
+        def _():
+            upper_detection()
+
+        for stage, lag in stages:
+            if lag >= 0:
+
+                @pl.when(jnp.logical_and(n >= lag, n < STEPS + lag))
+                def _():
+                    stage(n - lag, 0)
+
+            else:
+
+                @pl.when(n < STEPS + lag)
+                def _():
+                    stage(n - lag, 0)
+
+            if stage is make_template:
+
+                @pl.when(n == STEPS + 1)
+                def _():
+                    send_edges()
+
+        return 0
+
+    lax.fori_loop(0, AHEAD, stage_matched, 0)
+    lax.fori_loop(0, STEPS + 4, tick, 0)
+    lax.fori_loop(0, 1, subtract, 0)
     for step in range(1, STEPS):
         wait_for(natural.at[pl.ds(step * CHUNK, CHUNK)], x_sem.at[step])
     for i in range(5, 8):
@@ -590,26 +615,7 @@
     send_power(2)
     send_power(3)
 
-    def subtract(step, _):
-        for half in range(2):
-            wait_for(q_recv.at[pl.ds(1, 7), chunk_of(half, step)], q_sem.at[half, step])
-
-            def part(r, _):
-                at = strip_of(half, step, r)
-                tiles = []
-                for i in range(8):
-                    d = (8 - i) % 8
-                    m = m_send[i, at, :].astype(F32)
-                    q = (q_recv if d else q_send)[d, at, :].astype(F32)
-                    tiles.append((m - q).astype(BF16))
-                for c, tile in enumerate(turned(tiles, 64 - turn[half])):
-                    difference_out[at, c * TILE : (c + 1) * TILE] = tile
-                return 0
-
-            lax.fori_loop(0, CHUNK // 32, part, 0)
-        return 0
-
-    lax.fori_loop(0, STEPS, subtract, 0)
+    lax.fori_loop(1, STEPS, subtract, 0)
     wait_for(b_recv, b_sem)
     detection_out[...] = (
         power[quarter_of(band), :]
@@ -680,7 +686,7 @@
             pltpu.VMEM((3, IMG // 4, TILE), BF16),
             pltpu.SemaphoreType.DMA((3,)),
             pltpu.SemaphoreType.DMA((8,)),
-            arrivals,
+            pltpu.SemaphoreType.DMA((2,)),
             arrivals,
             arrivals,
             arrivals,

time: 69 us -> 66.6 us (0.965)
  Pallas kernels: 66.3 us -> 63.9 us
    pallas_call x1, Pallas kernels: 66.3 us -> 63.9 us  [coadd(): pl.pallas_call(coadd_kernel, out_shape=(pltpu.VMEM((IMG, IMG), BF16), plt...]
where the time goes in v5:
time: 66.6 us; the launch traced here: 66.5 us
  Pallas kernels  63.9 us (96%)
  local copies, waits for them, and re-layouts  1.98 us (3%)
    pallas_call x1, Pallas kernels, coadd(): pl.pallas_call(coadd_kernel, out_shape=(pltpu.VMEM((IMG, IMG), BF16), plt...  63.9 us
    unnamed x2, local copies, waits for them, and re-layouts  1.98 us

profile of v5, /device:TPU:6, one launch (start us, length us, event | category | flops | bytes accessed | tf_op | source)
XLA Modules:
  0.0 66.5 jit_solution(15555283858118241191)
XLA Ops:
  0.6 63.9 %coadd.1 = (bf16[1024,1024]{1,0:T(8,128)(2,1)S(1)}, f32[256,128]{1,0:T(8,128)S(1)}) custom-call(bf16[1024,1024]{1,0:T(8,128)(2,1)} %bitcast.7, bf16[1024,1024]{1,0:T(8,128)(2,1)} %bitcast.8, s32[2,35]{1,0:T(2,128)} %bitcast.10, s32[4,8,32]{2,1,0:T(8,128)} %bitcast.9, f32[9,25]{1,0:T(8,128)} %rows_ref.1, f32[9,25]{1,0:T(8,128)} %cols_ref.1, f32[1,9]{1,0:T(1,128)} %bitcast.11, ...), custom_call_target="tpu_custom_call" | custom-call | tf_op jit(solution)/shard_map/coadd/pallas_call | solution.py:650
  64.5 1.3 %copy.12 = bf16[1,1,1024,1024]{3,2,1,0:T(8,128)(2,1)} copy(bf16[1,1,1024,1024]{3,2,1,0:T(8,128)(2,1)S(1)} %bitcast.6) | data formatting | bytes 4194304
  65.8 0.7 copy.13

commit v6 on v5

--- a/solution.py
+++ b/solution.py
@@ -386,12 +386,9 @@
 
                 lax.fori_loop(0, HALF // 32, part, 0)
             after, before = ring[half][1], ring[half][3]
-            arrive = p_sem.at[half, step]
             onward = o_sem.at[half, step]
             send(p_send.at[2, piece, 0], o_recv.at[0, piece], send_sem.at[2], onward, after)
             send(p_send.at[2, piece, 1], o_recv.at[1, piece], send_sem.at[2], onward, before)
-            send(p_send.at[1, piece, 1], p_recv.at[0, piece, 1], send_sem.at[2], arrive, after)
-            send(p_send.at[3, piece, 0], p_recv.at[1, piece, 0], send_sem.at[2], arrive, before)
         return 0
 
     def combine(step, _):
@@ -405,8 +402,8 @@
                     ].astype(F32)
                     p_send[t, piece, top, kind] = total.astype(BF16)
                 send(
-                    p_send.at[t, piece, top],
-                    p_recv.at[side, piece, top],
+                    p_send.at[t, piece],
+                    p_recv.at[side, piece],
                     send_sem.at[2],
                     p_sem.at[half, step],
                     ring[half][t],
@@ -503,7 +500,7 @@
         return 0
 
     def subtract(step, _):
-        for half in range(2):
+        for half in (1, 0):
             wait_for(q_recv.at[pl.ds(1, 7), chunk_of(half, step)], q_sem.at[half, step])
 
             def part(r, _):

time: 66.6 us -> 66.5 us (level)
  the two profiles are of different devices: /device:TPU:6 before, /device:TPU:30 now
where the time goes in v6:
time: 66.5 us; the launch traced here: 66.3 us
  Pallas kernels  63.7 us (96%)
  local copies, waits for them, and re-layouts  1.98 us (3%)
    pallas_call x1, Pallas kernels, coadd(): pl.pallas_call(coadd_kernel, out_shape=(pltpu.VMEM((IMG, IMG), BF16), plt...  63.7 us
    unnamed x2, local copies, waits for them, and re-layouts  1.98 us

profile of v6, /device:TPU:30, one launch (start us, length us, event | category | flops | bytes accessed | tf_op | source)
XLA Modules:
  0.0 66.3 jit_solution(10726053469977913406)
XLA Ops:
  0.6 63.7 %coadd.1 = (bf16[1024,1024]{1,0:T(8,128)(2,1)S(1)}, f32[256,128]{1,0:T(8,128)S(1)}) custom-call(bf16[1024,1024]{1,0:T(8,128)(2,1)} %bitcast.7, bf16[1024,1024]{1,0:T(8,128)(2,1)} %bitcast.8, s32[2,35]{1,0:T(2,128)} %bitcast.10, s32[4,8,32]{2,1,0:T(8,128)} %bitcast.9, f32[9,25]{1,0:T(8,128)} %rows_ref.1, f32[9,25]{1,0:T(8,128)} %cols_ref.1, f32[1,9]{1,0:T(1,128)} %bitcast.11, ...), custom_call_target="tpu_custom_call" | custom-call | tf_op jit(solution)/shard_map/coadd/pallas_call | solution.py:647
  64.3 1.3 %copy.12 = bf16[1,1,1024,1024]{3,2,1,0:T(8,128)(2,1)} copy(bf16[1,1,1024,1024]{3,2,1,0:T(8,128)(2,1)S(1)} %bitcast.6) | data formatting | bytes 4194304
  65.6 0.7 copy.13
